TPU v7x, 32 devices: a whole 2x2x4 slice. The times are simulated.
32 devices in a mesh: dp: 4 (over x, core), seq: 2 (over y), fsdp: 4 (over z).
Axes of the slice: x: 2, y: 2, z: 4, core: 2. Of those that a mesh axis runs over, the one named last changes fastest.
Arguments:
- tokens: bfloat16 [16, 1536, 768], P(('dp', 'fsdp'), 'seq'), may hold values from -6 to 6
- attn_in: bfloat16 [768, 2304], P('fsdp'), may hold values from -0.21875 to 0.21875
- attn_out: bfloat16 [768, 768], P('fsdp'), may hold values from -1.75 to 1.75
- router: bfloat16 [768, 4], P('fsdp'), may hold values from -0.15625 to 0.15625
- gains: bfloat16 [768, 2], P('fsdp'), may hold values from 0.5 to 1.5
- expert_w: bfloat16 [3072, 4, 1536], P('fsdp'), may hold values from -0.21875 to 0.21875
- expert_ids: int32 [16, 1536, 2], P(('dp', 'fsdp'), 'seq'), may hold values from 0 to 3, all different within a row
- segments: int32 [16, 512], P(('dp', 'fsdp')), may hold values from 0 to 1, as said below
- cotangent: bfloat16 [16, 1536, 768], P(('dp', 'fsdp'), 'seq'), may hold values from -6 to 6
Outputs:
- block_out: bfloat16 [16, 1536, 768], P(('dp', 'fsdp'), 'seq')
- d_tokens: bfloat16 [16, 1536, 768], P(('dp', 'fsdp'), 'seq')
- d_attn_in: float32 [768, 2304], P('fsdp')
- d_attn_out: float32 [768, 768], P('fsdp')
- d_router: float32 [768, 4], P('fsdp')
- d_gains: float32 [768, 2], P('fsdp')
- d_expert: float32 [3072, 4, 1536], P('fsdp')
Inputs may be any that keep to these rules, and one draw needn't show every extreme that they name: `expert_ids`: the two experts of a token differ. `segments`: never falls along a group; every continuation has 64 to 384 tokens, and in every group one has exactly 384.
All inputs are finite; a program needn't handle non-finite values.
Results may differ from a plain program's by a relative error of at most 0.018.
Values may be sent and summed in bfloat16 or wider, within the bound.
A program may use at most 384 MiB of HBM per device.

v0:
```python
import functools

import jax
import jax.numpy as jnp
from jax import lax
from jax.experimental import pallas as pl
from jax.experimental.pallas import tpu as pltpu
from jax.sharding import PartitionSpec as P

HEADS = 12
HEAD_DIM = 64
EXPERTS = 4
PROMPT = 1024
EPSILON = 1e-06
NEGATIVE = -1e30
HIGH = lax.Precision.HIGHEST
LOG2E = 1.4426950408889634
BF = jnp.bfloat16
F32 = jnp.float32
MESH = pl.DeviceIdType.MESH
VMEM_LIMIT = 60 << 20
QB = 256
ANY = pl.BlockSpec(memory_space=pl.ANY)
VM = pl.BlockSpec(memory_space=pltpu.VMEM)


def nn(a, b):
    return lax.dot_general(a, b, (((1,), (0,)), ((), ())), preferred_element_type=F32)


def nt(a, b):
    return lax.dot_general(a, b, (((1,), (1,)), ((), ())), preferred_element_type=F32)


def tn(a, b):
    return lax.dot_general(a, b, (((0,), (0,)), ((), ())), preferred_element_type=F32)


def iota(shape, dim):
    return lax.broadcasted_iota(jnp.int32, shape, dim)


def params(cid=None):
    if cid is None:
        return pltpu.CompilerParams(vmem_limit_bytes=VMEM_LIMIT)
    return pltpu.CompilerParams(
        vmem_limit_bytes=VMEM_LIMIT, collective_id=cid, has_side_effects=True
    )


def sds(shape, dtype):
    return jax.ShapeDtypeStruct(shape, dtype)


def place():
    dp, sq, z = lax.axis_index("dp"), lax.axis_index("seq"), lax.axis_index("fsdp")
    return dp, sq, z, dp // 2, lax.rem(dp, 2)


def greet(peers):
    barrier = pltpu.get_barrier_semaphore()
    for peer in peers:
        pl.semaphore_signal(barrier, inc=1, device_id=peer, device_id_type=MESH)
    pl.semaphore_wait(barrier, len(peers))


def remote(src, dst, send, recv, peer):
    return pltpu.make_async_remote_copy(
        src_ref=src, dst_ref=dst, send_sem=send, recv_sem=recv, device_id=peer, device_id_type=MESH
    )


def al(x):
    return pl.multiple_of(x, 128)


def allowed_tile(j, i, prompt, seg_col, seg_row):
    mask = None
    if i == j:
        mask = iota((QB, QB), 0) <= iota((QB, QB), 1)
    if j * QB >= prompt:
        keys, queries = j * QB - prompt, i * QB - prompt
        same = seg_col[keys : keys + QB, :] == seg_row[:, queries : queries + QB]
        mask = same if mask is None else mask & same
    return mask


def flip_chip(x, sq, fx, fy):
    px = 1 - x if fx else x
    py = 1 - sq if fy else sq
    return px, py


SOURCES = ((1, 0), (0, 1), (0, 0), (1, 1))
OWN = 2
AWAY = (0, 1, 3)


class Line:
    def __init__(self, nz, dp, sq, z, sources, target, sems):
        self.nz, self.dp, self.sq, self.z = nz, dp, sq, z
        self.sources, self.target, self.sems = sources, target, sems

    def copy(self, stage, up):
        nz, z = self.nz, self.z
        zone = z - (stage - 1) if up else z + (stage - 1)
        zone = lax.rem(zone + nz, nz)
        to = lax.rem(z + 1, nz) if up else lax.rem(z + nz - 1, nz)
        i = stage - 1
        send, recv = (self.sems[0], self.sems[1]) if up else (self.sems[2], self.sems[3])
        return remote(
            self.sources(stage, zone), self.target.at[zone], send.at[i], recv.at[i], (self.dp, self.sq, to)
        )

    def arrival(self, stage, up):
        nz, z = self.nz, self.z
        zone = lax.rem((z - stage if up else z + stage) + nz, nz)
        to = lax.rem(z + 1, nz) if up else lax.rem(z + nz - 1, nz)
        i = stage - 1
        send, recv = (self.sems[0], self.sems[1]) if up else (self.sems[2], self.sems[3])
        return remote(
            self.sources(stage, zone), self.target.at[zone], send.at[i], recv.at[i], (self.dp, self.sq, to)
        )

    def sends(self, stage, up):
        z, nz = self.z, self.nz
        return (z < nz - 1) & (z >= stage - 1) if up else (z > 0) & (z <= nz - stage)

    def gets(self, stage, up):
        return self.z >= stage if up else self.z <= self.nz - 1 - stage

    def start(self, stage):
        for up in (True, False):

            @pl.when(self.sends(stage, up))
            def _(up=up):
                self.copy(stage, up).start()

    def wait_recv(self, stage):
        for up in (True, False):

            @pl.when(self.gets(stage, up))
            def _(up=up):
                self.arrival(stage, up).wait_recv()

    def wait_send(self, stage):
        for up in (True, False):

            @pl.when(self.sends(stage, up))
            def _(up=up):
                self.copy(stage, up).wait_send()


def eighth(x, prompt):
    row = x.astype(F32)
    col = jnp.broadcast_to(row, (128, row.shape[1])).T[:, 0:1]
    return row, col


def begin_kernel(
    prompt, nz, capacity, x_ref, in_ref, out_ref, router_ref, gains_ref, seg_ref, ids_ref, cot_ref, piece_ref,
    xs_ref, w_ref, qkv_ref, mixed_ref, lse_ref, att_ref, raw_ref, row_ref, col_ref, near_ref,
    pack, vt, local, send_t, recv_t, send_z, recv_z, send_p, recv_p, send_c, recv_c, send_o, recv_o, *line_sems,
):
    dp, sq, z, x, core = place()
    rows, width = x_ref.shape
    shard = in_ref.shape[0]
    part = shard // 4
    half = width // 2
    pairs = half // 128
    own_cols = 3 * half
    lead = own_cols + 128
    sibling = (x * 2 + 1 - core, sq, z)
    partner = (dp, 1 - sq, z)
    across = ((1 - x) * 2 + core, sq, z)
    others = [(dp, sq, lax.rem(z + d, nz)) for d in range(1, nz)]
    base = pl.multiple_of(sq * rows, rows)
    there = pl.multiple_of((1 - sq) * rows, rows)
    groups = (pl.ds(0, lead), pl.ds(lead, width))

    packs = [
        pltpu.make_async_copy(
            in_ref.at[:, pl.ds(al(i * width + sq * half), half)], pack.at[:, pl.ds(i * half, half)], local.at[i]
        )
        for i in range(3)
    ]
    packs.append(pltpu.make_async_copy(out_ref, pack.at[:, groups[1]], local.at[3]))
    for c in packs:
        c.start()
    lane = iota((1, 128), 1)
    small = jnp.zeros((shard, 128), F32)
    for e in range(EXPERTS):
        small = jnp.where(lane == e, router_ref[:, e : e + 1].astype(F32), small)
    for e in range(2):
        small = jnp.where(lane == EXPERTS + e, gains_ref[:, e : e + 1].astype(F32), small)
    pack[:, own_cols:lead] = small.astype(BF)
    greet([sibling, partner, across] + others)
    tokens = remote(x_ref, xs_ref.at[pl.ds(base, rows)], send_t, recv_t, partner)
    tokens.start()
    for c in packs:
        c.wait()

    def at(zs, px, co, g):
        return w_ref.at[pl.ds(pl.multiple_of(zs * shard + (px * 2 + co) * part, part), part), groups[g]]

    def along(d, g):
        src = pack.at[pl.ds(pl.multiple_of((x * 2 + core) * part, part), part), groups[g]]
        return remote(src, at(z, x, core, g), send_z.at[d - 1, g], recv_z.at[d - 1, g], others[d - 1])

    def source(d):
        return lax.rem(z + nz - d, nz)

    def over(d, g, px):
        ref = at(source(d), px, core, g)
        return remote(ref, ref, send_p.at[d - 1, g], recv_p.at[d - 1, g], across)

    def beside(d, g, i, co):
        ref = at(source(d), (x, 1 - x)[i], co, g)
        return remote(ref, ref, send_c.at[d - 1, g, i], recv_c.at[d - 1, g, i], sibling)

    for d in range(1, nz):
        along(d, 0).start()
    own = pltpu.make_async_copy(pack, w_ref.at[pl.ds(pl.multiple_of(z * shard, shard), shard)], local.at[4])
    own.start()
    xs_ref[pl.ds(base, rows), :] = x_ref[...]
    ids = ids_ref[...]
    chosen = jnp.where((ids[:, 0:1] == lane) | (ids[:, 1:2] == lane), 1.0, 0.0)
    earlier = (iota((rows, rows), 1) < iota((rows, rows), 0)).astype(F32).astype(BF)
    places = jnp.where(chosen > 0, nn(earlier, chosen.astype(BF)), -1.0)
    col_ref[...] = places
    places = places.T[0:8, :]
    row_ref[...] = places

    def gather(g):
        for d in range(1, nz):
            along(d, g).wait_recv()
            over(d, g, x).start()
            beside(d, g, 0, core).start()
        if g == 0:
            line.start(1)
            for d in range(1, nz):
                along(d, 1).start()
        for d in range(1, nz):
            over(d, g, 1 - x).wait_recv()
            beside(d, g, 1, core).start()

    def gathered(g):
        for d in range(1, nz):
            for i in range(2):
                beside(d, g, i, 1 - core).wait_recv()

    stay = pltpu.make_async_copy(piece_ref, near_ref.at[z], local.at[5])
    stay.start()
    line = Line(
        nz, dp, sq, z, lambda stage, zone: piece_ref if stage == 1 else near_ref.at[zone], near_ref, line_sems
    )
    gather(0)
    gathered(0)
    own.wait()
    tokens.wait_recv()

    gain = w_ref[:, own_cols:lead].astype(F32).T[EXPERTS : EXPERTS + 1, :]
    xf = xs_ref[...].astype(F32)
    normed = (xf * lax.rsqrt(jnp.mean(xf * xf, axis=1, keepdims=True) + EPSILON) * gain).astype(BF)
    for i in range(3):
        got = nn(normed, w_ref[:, i * half : (i + 1) * half]).astype(BF)
        for p in range(pairs):
            qkv_ref[p, i] = got[:, p * 128 : (p + 1) * 128]

    blocks = 2 * rows // QB
    const = HEAD_DIM ** (-0.5) * LOG2E
    seg_row, seg_col = eighth(seg_ref[...], prompt)

    def back(p, own_side):
        src = mixed_ref.at[p, pl.ds(there, rows)]
        side = sq if own_side else 1 - sq
        return remote(
            src, att_ref.at[:, pl.ds(al(side * half + p * 128), 128)], send_o.at[p], recv_o.at[p], partner
        )

    @pl.loop(0, pairs)
    def _(p):
        vt[0:128, :] = qkv_ref[p, 2].T
        vt[128:144, :] = jnp.ones((16, vt.shape[1]), BF)
        for i in range(blocks):
            here = slice(i * QB, (i + 1) * QB)
            both = []
            for h in range(2):
                lanes = iota((1, 128), 1) // HEAD_DIM == h
                q = jnp.where(lanes, qkv_ref[p, 0, here, :], jnp.zeros((), BF))
                tiles = []
                for j in range(i + 1):
                    s = nt(qkv_ref[p, 1, j * QB : (j + 1) * QB, :], q)
                    mask = allowed_tile(j, i, prompt, seg_col, seg_row)
                    if mask is not None:
                        s = jnp.where(mask, s, NEGATIVE)
                    tiles.append(s)
                top = functools.reduce(
                    jnp.maximum, [jnp.max(s, axis=0, keepdims=True) for s in tiles]
                )
                top = top * const
                acc = None
                for j, s in enumerate(tiles):
                    pr = jnp.exp2(s * const - top).astype(BF)
                    add = nn(vt[:, j * QB : (j + 1) * QB], pr)
                    acc = add if acc is None else acc + add
                total = acc[128:129, :]
                lse_ref[p, h : h + 1, here] = top + jnp.log2(total)
                low = h * HEAD_DIM
                both.append(acc[low : low + HEAD_DIM, :] * (1.0 / total))
            mixed_ref[p, here, :] = jnp.concatenate(both, axis=0).T.astype(BF)
        back(p, True).start()
        att_ref[:, pl.ds(al(sq * half + p * 128), 128)] = mixed_ref[p, pl.ds(base, rows), :]

        @pl.when(p == 0)
        def _():
            line.wait_recv(1)
            line.start(2)
            gather(1)

    for j, (px, py) in enumerate([flip_chip(x, sq, *f) for f in SOURCES]):
        hot = hot_rows(pick_row(row_ref[...], px * 2 + py), capacity)
        raw_ref[j] = nn(hot, cot_ref[...]).astype(BF)
    for p in range(pairs):
        back(p, False).wait_recv()
        back(p, True).wait_send()
    gathered(1)
    tokens.wait_send()
    for g in range(2):
        for d in range(1, nz):
            along(d, g).wait_send()
            over(d, g, x).wait_send()
            for i in range(2):
                beside(d, g, i, core).wait_send()
    line.wait_recv(2)
    line.wait_send(1)
    line.wait_send(2)
    stay.wait()


def begin(x, attn_in, attn_out, router, gains, segments, ids, cot, piece, prompt, nz, capacity, cid):
    rows, width = x.shape
    shard = attn_in.shape[0]
    pairs = width // 256
    cols = 3 * width // 2 + 128 + width
    dma = pltpu.SemaphoreType.DMA
    two = lambda *shape: [dma(shape), dma(shape)]
    return pl.pallas_call(
        functools.partial(begin_kernel, prompt, nz, capacity),
        out_shape=(
            sds((2 * rows, width), BF),
            sds((shard * nz, cols), BF),
            sds((pairs, 3, 2 * rows, 128), BF),
            sds((pairs, 2 * rows, 128), BF),
            sds((pairs, 8, 2 * rows), F32),
            sds((rows, width), BF),
            sds((4, capacity, width), BF),
            sds((8, rows), F32),
            sds((rows, 128), F32),
            sds((nz,) + piece.shape, BF),
        ),
        in_specs=[VM, ANY, ANY, VM, VM, VM, VM, VM, ANY],
        out_specs=(VM,) * 9 + (ANY,),
        scratch_shapes=[
            pltpu.VMEM((shard, cols), BF),
            pltpu.VMEM((144, 2 * rows), BF),
            dma((6,)),
        ]
        + two() + two(nz - 1, 2) + two(nz - 1, 2) + two(nz - 1, 2, 2) + two(pairs) + two(2) + two(2),
        compiler_params=params(cid),
        name="begin",
    )(x, attn_in, attn_out, router, gains, segments, ids, cot, piece)


def softmax_lanes(logits):
    live = iota(logits.shape, 1) < EXPERTS
    logits = jnp.where(live, logits, NEGATIVE)
    expo = jnp.where(live, jnp.exp(logits - jnp.max(logits, axis=1, keepdims=True)), 0.0)
    return expo / jnp.sum(expo, axis=1, keepdims=True)


def pick_row(table, e):
    return jnp.sum(jnp.where(iota((8, 1), 0) == e, table, 0.0), axis=0, keepdims=True)


def pick_col(table, e):
    return jnp.sum(jnp.where(iota((1, 128), 1) == e, table, 0.0), axis=1, keepdims=True)


def hot_rows(row, capacity):
    return (row == iota((capacity, 1), 0).astype(F32)).astype(F32).astype(BF)


def hot_cols(col, capacity):
    return (col == iota((1, capacity), 1).astype(F32)).astype(F32).astype(BF)


GELU_A = 0.7978845608028654
GELU_B = GELU_A * 0.044715


def expert_step(x, g, w):
    width = x.shape[1]
    first, second = w[:, :width], w[:, width:]
    pre = nt(x, first)
    back = nt(g, second)
    square = pre * pre
    t = jnp.tanh(pre * (GELU_A + GELU_B * square))
    rise = 0.5 + 0.5 * t
    act = (pre * rise).astype(BF)
    slope = rise + (0.5 * pre) * (1.0 - t * t) * (GELU_A + (3.0 * GELU_B) * square)
    grad_pre = (back * slope).astype(BF)
    return nn(act, second), nn(grad_pre, first), tn(grad_pre, x), tn(act, g)


def experts_kernel(
    capacity, nz, x_ref, att_ref, w_hbm, places_row, places_col, raw_send, near_ref,
    hidden_ref, probs_ref, back_gin, out_res, back_dot, dw_ref,
    wp, send_in, got_in, send_gate, got_gate, own_w, theirs, grad, res_acc, gin_acc, out_gin, out_dot, dw_away, dw_got,
    raw_ref, local, send_x, recv_x, send_w, recv_w, send_i, recv_i, send_t, recv_t, send_r, recv_r, send_d, recv_d, send_v, recv_v, *line_sems,
):
    dp, sq, z, x, core = place()
    rows, width = x_ref.shape
    sibling = (x * 2 + 1 - core, sq, z)
    corner = [flip_chip(x, sq, *f) for f in SOURCES]
    plane = [(px * 2 + core, py, z) for px, py in corner]
    experts_of = [px * 2 + py for px, py in corner]
    below, above = (dp, sq, lax.rem(z + nz - 1, nz)), (dp, sq, lax.rem(z + 1, nz))
    shift = jnp.where(z >= nz // 2, 1, 0)
    far_zone = jnp.where(z >= nz // 2, 0, nz - 1)
    greet([sibling, below, above] + [plane[j] for j in AWAY])
    line = Line(nz, dp, sq, z, lambda stage, zone: near_ref.at[zone], own_w, line_sems)
    line.start(nz - 1)
    at_end = (z == 0) | (z == nz - 1)

    def go_raw(j):
        return remote(raw_send.at[j], raw_ref.at[j], send_x.at[j], recv_x.at[j], plane[j])

    go_raw(0).start()
    go_raw(1).start()

    def weights(slot):
        if slot == nz - 1:
            return remote(own_w.at[far_zone], theirs.at[far_zone], send_w.at[slot], recv_w.at[slot], sibling)
        zone = slot + shift
        return remote(near_ref.at[zone], theirs.at[zone], send_w.at[slot], recv_w.at[slot], sibling)

    lifts = []
    for i in range(nz - 1):
        weights(i).start()
        lifts.append(pltpu.make_async_copy(near_ref.at[i + shift], own_w.at[i + shift], local.at[2 + i]))
    for c in lifts:
        c.start()
    far_lift = pltpu.make_async_copy(near_ref.at[far_zone], own_w.at[far_zone], local.at[1 + nz])

    @pl.when(jnp.logical_not(at_end))
    def _():
        far_lift.start()

    own_raw = pltpu.make_async_copy(raw_send.at[OWN], raw_ref.at[OWN], local.at[1])
    own_raw.start()
    load = pltpu.make_async_copy(w_hbm.at[:, 3 * width // 2 :], wp, local.at[0])
    load.start()
    load.wait()

    hidden = x_ref[...].astype(F32) + nn(att_ref[...], wp[:, 128:])
    hidden_ref[...] = hidden
    r_two = lax.rsqrt(jnp.mean(hidden * hidden, axis=1, keepdims=True) + EPSILON)
    small = wp[:, :128]
    gain = small.astype(F32).T[EXPERTS + 1 : EXPERTS + 2, :]
    routed = (hidden * r_two * gain).astype(BF)
    probs = softmax_lanes(nn(routed, small))
    probs_ref[...] = probs
    flat = probs.T[0:8, :]
    high = flat.astype(BF)
    rest = flat - high.astype(F32)
    mid = rest.astype(BF)
    low = (rest - mid.astype(F32)).astype(BF)
    split = jnp.concatenate([high.astype(F32), mid.astype(F32), low.astype(F32)], axis=0).astype(BF)

    def go_in(j):
        return remote(send_in.at[j], got_in.at[j], send_i.at[j], recv_i.at[j], plane[j])

    def go_gate(j):
        return remote(send_gate.at[j], got_gate.at[j], send_t.at[j], recv_t.at[j], plane[j])

    for j in range(4):
        e = experts_of[j]
        taken = nn(hot_rows(pick_row(places_row[...], e), capacity), routed).astype(BF)
        three = nn(split, hot_cols(pick_col(places_col[...], e), capacity))
        gate = three[0:8] + three[8:16] + three[16:24]
        gate = jnp.broadcast_to(pick_row(gate, e), gate.shape)
        if j != OWN:
            send_in[j] = taken
            send_gate[j] = gate
            go_gate(j).start()
        if j < OWN:
            go_in(j).start()
        if j == OWN:
            got_in[j] = taken
            got_gate[j] = gate
    own_raw.wait()
    for c in lifts:
        c.wait()
    for i in range(nz - 1):
        weights(i).wait_recv()

    def go_gin(j):
        return remote(out_gin.at[j], back_gin.at[j], send_r.at[j], recv_r.at[j], plane[j])

    def go_dot(j):
        return remote(out_dot.at[j], back_dot.at[j], send_d.at[j], recv_d.at[j], plane[j])

    def go_dw(n):
        return remote(dw_away.at[n], dw_got.at[n], send_v.at[n], recv_v.at[n], sibling)

    def arrive(lo, hi):
        for j in range(lo, hi):
            if j != OWN:
                go_raw(j).wait_recv()
                go_in(j).wait_recv()
                go_gate(j).wait_recv()
            gate = got_gate[j].T[:, 0:1]
            grad[j] = (raw_ref[j].astype(F32) * gate).astype(BF)

    def chunk(lo, hi, w_ref, dw, d, first, at):
        count = (hi - lo) * capacity
        xs = got_in[lo:hi].reshape(count, width)
        gs = grad[lo:hi].reshape(count, width)
        res, gin, d_first, d_second = expert_step(xs, gs, w_ref[d])
        here = slice(at * capacity, at * capacity + count)
        res_acc[here, :] += res
        gin_acc[here, :] += gin
        if first:
            dw[d, :, :width] = d_first.astype(BF)
            dw[d, :, width:] = d_second.astype(BF)
        else:
            dw[d, :, :width] = (dw[d, :, :width].astype(F32) + d_first).astype(BF)
            dw[d, :, width:] = (dw[d, :, width:].astype(F32) + d_second).astype(BF)

    def send_back(lo, hi, at):
        for j in range(lo, hi):
            here = slice((at + j - lo) * capacity, (at + j - lo + 1) * capacity)
            prod = res_acc[here, :] * raw_ref[j].astype(F32)
            narrow = functools.reduce(jnp.add, [prod[:, i : i + 128] for i in range(0, width, 128)])
            inner = jnp.broadcast_to(jnp.sum(narrow.T, axis=0, keepdims=True), (8, capacity))
            if j != OWN:
                out_gin[j] = gin_acc[here, :].astype(BF)
                out_dot[j] = inner
                go_gin(j).start()
                go_dot(j).start()
            else:
                back_gin[j] = gin_acc[here, :].astype(BF)
                back_dot[j] = inner
        for j in range(lo, hi):
            here = slice((at + j - lo) * capacity, (at + j - lo + 1) * capacity)
            out_res[j] = res_acc[here, :].astype(BF)

    both = ((theirs, dw_away), (own_w, dw_ref))
    res_acc[...] = jnp.zeros(res_acc.shape, F32)
    gin_acc[...] = jnp.zeros(gin_acc.shape, F32)
    arrive(OWN, OWN + 1)
    for w_ref, dw in both:

        @pl.loop(0, nz - 1)
        def _(i):
            chunk(OWN, OWN + 1, w_ref, dw, i + shift, True, OWN)

    arrive(0, OWN)
    go_raw(3).start()
    go_in(3).start()
    for w_ref, dw in both:

        @pl.loop(0, nz - 1)
        def _(i):
            chunk(0, OWN, w_ref, dw, i + shift, False, 0)

    @pl.when(jnp.logical_not(at_end))
    def _():
        far_lift.wait()

    line.wait_recv(nz - 1)
    weights(nz - 1).start()
    chunk(0, OWN + 1, own_w, dw_ref, far_zone, True, 0)
    weights(nz - 1).wait_recv()
    chunk(0, OWN + 1, theirs, dw_away, far_zone, True, 0)
    send_back(0, OWN + 1, 0)
    arrive(3, 4)
    res_acc[0:capacity, :] = jnp.zeros((capacity, width), F32)
    gin_acc[0:capacity, :] = jnp.zeros((capacity, width), F32)

    @pl.loop(0, nz)
    def _(d):
        chunk(3, 4, theirs, dw_away, d, False, 0)
        go_dw(d).start()

    @pl.loop(0, nz)
    def _(d):
        chunk(3, 4, own_w, dw_ref, d, False, 0)

    send_back(3, 4, 0)
    for n in range(nz):
        go_dw(n).wait_recv()
        dw_ref[n] = (dw_ref[n].astype(F32) + dw_got[n].astype(F32)).astype(BF)
    for j in AWAY:
        go_gin(j).wait_recv()
        go_dot(j).wait_recv()
    line.wait_send(nz - 1)
    for n in range(nz):
        weights(n).wait_send()
        go_dw(n).wait_send()
    for j in AWAY:
        for c in (go_raw(j), go_in(j), go_gate(j), go_gin(j), go_dot(j)):
            c.wait_send()


def experts(x, attended, whole, places_row, places_col, raw, near, capacity, nz, cid):
    rows, width = x.shape
    part = near.shape[1]
    slots = sds((4, capacity, width), BF)
    small = sds((4, 8, capacity), F32)
    dma = pltpu.SemaphoreType.DMA
    two = lambda *shape: [dma(shape), dma(shape)]
    vm = pltpu.VMEM
    return pl.pallas_call(
        functools.partial(experts_kernel, capacity, nz),
        out_shape=(
            sds((rows, width), F32),
            sds((rows, 128), F32),
            slots,
            slots,
            small,
            sds((nz, part, 2 * width), BF),
        ),
        in_specs=[VM, VM, ANY, VM, VM, ANY, ANY],
        out_specs=(VM,) * 6,
        scratch_shapes=[
            vm((rows, width + 128), BF),
            vm((4, capacity, width), BF),
            vm((4, capacity, width), BF),
            vm((4, 8, capacity), F32),
            vm((4, 8, capacity), F32),
            vm((nz, part, 2 * width), BF),
            vm((nz, part, 2 * width), BF),
            vm((4, capacity, width), BF),
            vm((3 * capacity, width), F32),
            vm((3 * capacity, width), F32),
            vm((4, capacity, width), BF),
            vm((4, 8, capacity), F32),
            vm((nz, part, 2 * width), BF),
            vm((nz, part, 2 * width), BF),
            vm((4, capacity, width), BF),
            dma((2 + nz,)),
        ]
        + two(4) + two(nz) + two(4) + two(4) + two(4) + two(4) + two(nz) + two(nz - 1) + two(nz - 1),
        compiler_params=params(cid),
        name="experts",
    )(x, attended, whole, places_row, places_col, raw, near)


def after_kernel(
    capacity, nz, gin_ref, res_ref, dot_ref, hidden_ref, probs_ref, places_col, cot_ref, w_hbm, att_ref, part_ref,
    out_ref, gh_ref, gatt_ref, dw_ref, dr_ref, dg_ref, got_ref,
    wp, got_res, local, send, recv, send_z, recv_z,
):
    dp, sq, z, x, core = place()
    rows, width = hidden_ref.shape
    corner = [flip_chip(x, sq, *f) for f in SOURCES]
    plane = [(px * 2 + core, py, z) for px, py in corner]
    experts_of = [px * 2 + py for px, py in corner]
    others = [(dp, sq, lax.rem(z + d, nz)) for d in range(1, nz)]
    greet([plane[j] for j in AWAY] + others)
    first = pl.ds(0, got_ref.shape[1])
    zones = [
        remote(part_ref.at[lax.rem(z + d, nz), first], got_ref.at[d - 1], send_z.at[d - 1], recv_z.at[d - 1], others[d - 1])
        for d in range(1, nz)
    ]
    for c in zones:
        c.start()
    copies = {j: remote(res_ref.at[j], got_res.at[j], send.at[j], recv.at[j], plane[j]) for j in AWAY}
    for c in copies.values():
        c.start()
    load = pltpu.make_async_copy(w_hbm.at[:, 3 * width // 2 :], wp, local)
    load.start()
    load.wait()
    hidden = hidden_ref[...]
    probs = probs_ref[...]
    small = wp[:, :128]
    gain = small.astype(F32).T[EXPERTS + 1 : EXPERTS + 2, :]
    lane = iota(probs.shape, 1)
    back = None
    grad_probs = jnp.zeros_like(probs)
    for j in range(4):
        pick = hot_cols(pick_col(places_col[...], experts_of[j]), capacity)
        part = nn(pick, gin_ref[j])
        back = part if back is None else back + part
        inner = jnp.sum(pick.astype(F32) * dot_ref[j][0:1, :], axis=1, keepdims=True)
        grad_probs = jnp.where(lane == experts_of[j], inner, grad_probs)
    mixed = jnp.sum(probs * grad_probs, axis=1, keepdims=True)
    low = (probs * (grad_probs - mixed)).astype(BF)
    r_two = lax.rsqrt(jnp.mean(hidden * hidden, axis=1, keepdims=True) + EPSILON)
    h_norm = hidden * r_two
    routed = (h_norm * gain).astype(BF)
    grad_routed = back + nt(low, small)
    dg_ref[...] = jnp.sum(grad_routed * h_norm, axis=0, keepdims=True)
    u = grad_routed * gain
    grad_hidden = cot_ref[...].astype(F32) + r_two * (
        u - h_norm * jnp.mean(u * h_norm, axis=1, keepdims=True)
    )
    gh_ref[...] = grad_hidden
    hid_low = grad_hidden.astype(BF)
    gatt_ref[...] = nt(hid_low, wp[:, 128:]).astype(BF)
    dr_ref[...] = tn(routed, low)
    dw_ref[...] = tn(att_ref[...], hid_low).astype(BF)
    total = hidden
    for j in (OWN,) + AWAY:
        if j != OWN:
            copies[j].wait_recv()
        value = res_ref[j] if j == OWN else got_res[j]
        pick = hot_cols(pick_col(places_col[...], experts_of[j]), capacity)
        total = total + pick_col(probs, experts_of[j]) * nn(pick, value)
    out_ref[...] = total.astype(BF)
    for c in copies.values():
        c.wait_send()
    for c in zones:
        c.wait()


def after(gin, res, inner, hidden, probs, places_col, cot, whole, attended, dw_half, capacity, cid):
    nz, part, deep = dw_half.shape
    rows, width = hidden.shape
    dma = pltpu.SemaphoreType.DMA
    return pl.pallas_call(
        functools.partial(after_kernel, capacity, nz),
        out_shape=(
            sds((rows, width), BF),
            sds((rows, width), F32),
            sds((rows, width), BF),
            sds((width, width), BF),
            sds((width, 128), F32),
            sds((1, width), F32),
            sds((nz - 1, part // PARTS, deep), BF),
        ),
        in_specs=[VM] * 7 + [ANY, VM, ANY],
        out_specs=(VM,) * 6 + (ANY,),
        scratch_shapes=[
            pltpu.VMEM((rows, width + 128), BF),
            pltpu.VMEM((4, capacity, width), BF),
            dma(()),
            dma((4,)),
            dma((4,)),
            dma((nz - 1,)),
            dma((nz - 1,)),
        ],
        compiler_params=params(cid),
        name="after",
    )(gin, res, inner, hidden, probs, places_col, cot, whole, attended, dw_half)


PARTS = 4


def finish_kernel(
    prompt, nz, xs_ref, gatt_ref, qkv_ref, mixed_ref, lse_ref, w_ref, gh_ref, dout_ref, droute_ref, dgain_ref,
    seg_ref, part_ref, got_first,
    dx_ref, din_out, dout_out, droute_out, dgains_out, got_rest, dw_all,
    grad, qm, dom, kt, dqt, dcat, norm_t, sums, got_c, got_x, got_z, mine, fin, got_f, total, send_dx, got_dx, own_gn,
    stage, dw_sum,
    local, send_g, recv_g, send_c, recv_c, send_x, recv_x, send_z, recv_z, send_d, recv_d, send_f, recv_f,
    send_a, recv_a, send_b, recv_b, send_s, recv_s, send_v, recv_v, send_h, recv_h, send_k, recv_k,
):
    dp, sq, z, x, core = place()
    rows, width = gatt_ref.shape
    half = width // 2
    pairs = half // 128
    shard = width // nz
    part = shard // 4
    own_cols = 3 * half
    lead = own_cols + 128
    chip = x * 2 + sq
    chip_x, chip_y, chip_d = (1 - x) * 2 + sq, x * 2 + 1 - sq, (1 - x) * 2 + 1 - sq
    sibling = (x * 2 + 1 - core, sq, z)
    partner = (dp, 1 - sq, z)
    across = ((1 - x) * 2 + core, sq, z)
    others = [(dp, sq, lax.rem(z + d, nz)) for d in range(1, nz)]
    base = pl.multiple_of(sq * rows, rows)
    there = pl.multiple_of((1 - sq) * rows, rows)
    greet([sibling, partner, across] + others)

    quarter = got_first.shape[1]

    def zone_part(k, d):
        return remote(
            part_ref.at[lax.rem(z + d, nz), pl.ds(k * quarter, quarter)],
            got_rest.at[k - 1, d - 1],
            send_s.at[k - 1, d - 1],
            recv_s.at[k - 1, d - 1],
            others[d - 1],
        )

    def share(k, ch, send, recv, peer, own=False):
        at = dw_all.at[core, ch, pl.ds(k * quarter, quarter)]
        return remote(dw_sum.at[k] if own else at, at, send, recv, peer)

    def keep(k):
        return pltpu.make_async_copy(
            dw_sum.at[k], dw_all.at[core, chip, pl.ds(k * quarter, quarter)], local.at[nz + k]
        )

    def start_part(k):
        for d in range(1, nz):
            zone_part(k, d).start()

    def sum_part(k):
        loads = []
        for d in range(nz - 1):
            if k > 0:
                zone_part(k, d + 1).wait_recv()
            src = got_first.at[d] if k == 0 else got_rest.at[k - 1, d]
            loads.append(pltpu.make_async_copy(src, stage.at[d], local.at[d]))
        loads.append(
            pltpu.make_async_copy(part_ref.at[z, pl.ds(k * quarter, quarter)], stage.at[nz - 1], local.at[nz - 1])
        )
        for c in loads:
            c.start()
        for c in loads:
            c.wait()
        acc = stage[0].astype(F32)
        for d in range(1, nz):
            acc = acc + stage[d].astype(F32)
        dw_sum[k] = acc.astype(BF)
        share(k, chip, send_v.at[k], recv_v.at[k], partner, True).start()
        share(k, chip, send_h.at[k, 0], recv_h.at[k, 0], across, True).start()
        share(k, chip, send_k.at[k, 0], recv_k.at[k, 0], sibling, True).start()
        keep(k).start()

    def pass_part(k):
        share(k, chip_y, send_v.at[k], recv_v.at[k], partner).wait_recv()
        share(k, chip_y, send_h.at[k, 1], recv_h.at[k, 1], across).start()
        share(k, chip_y, send_k.at[k, 1], recv_k.at[k, 1], sibling).start()

    def last_part(k):
        share(k, chip_x, send_h.at[k, 0], recv_h.at[k, 0], across).wait_recv()
        share(k, chip_x, send_k.at[k, 2], recv_k.at[k, 2], sibling).start()
        share(k, chip_d, send_h.at[k, 1], recv_h.at[k, 1], across).wait_recv()
        share(k, chip_d, send_k.at[k, 3], recv_k.at[k, 3], sibling).start()

    def end_part(k):
        other = [chip, chip_y, chip_x, chip_d]
        for i in range(4):
            at = dw_all.at[1 - core, other[i], pl.ds(k * quarter, quarter)]
            remote(at, at, send_k.at[k, i], recv_k.at[k, i], sibling).wait_recv()
            share(k, other[i], send_k.at[k, i], recv_k.at[k, i], sibling, i == 0).wait_send()
        share(k, chip, send_v.at[k], recv_v.at[k], partner, True).wait_send()
        share(k, chip, send_h.at[k, 0], recv_h.at[k, 0], across, True).wait_send()
        share(k, chip_y, send_h.at[k, 1], recv_h.at[k, 1], across).wait_send()
        keep(k).wait()
        if k > 0:
            for d in range(1, nz):
                zone_part(k, d).wait_send()

    groups = (pl.ds(0, lead), pl.ds(lead, width))
    order = [lax.rem(z + d, nz) for d in range(1, nz + 1)]

    def piece(zz, px, co):
        return pl.ds(pl.multiple_of(zz * shard + (px * 2 + co) * part, part), part)

    def to_core(g, n, i):
        src = sums.at[piece(order[n], (1 - x, x)[i], 1 - core), groups[g]]
        return remote(src, got_c.at[n, i, :, groups[g]], send_c.at[g, n, i], recv_c.at[g, n, i], sibling)

    def to_x(g, n):
        src = sums.at[piece(order[n], 1 - x, core), groups[g]]
        return remote(src, got_x.at[n, :, groups[g]], send_x.at[g, n], recv_x.at[g, n], across)

    def to_z(g, n):
        return remote(
            mine.at[n, :, groups[g]], got_z.at[n, :, groups[g]], send_z.at[g, n], recv_z.at[g, n], others[n]
        )

    def cols_of(g):
        return slice(0, lead) if g == 0 else slice(lead, lead + width)

    def reduce_core(g, n):
        cols = cols_of(g)
        for i in range(2):
            to_core(g, n, i).wait_recv()
            at = piece(order[n], (1 - x, x)[i], core)
            sums[at, cols] = (sums[at, cols].astype(F32) + got_c[n, i, :, cols].astype(F32)).astype(BF)
            if i == 0:
                to_x(g, n).start()

    def reduce_x(g, n):
        cols = cols_of(g)
        to_x(g, n).wait_recv()
        acc = sums[piece(order[n], x, core), cols].astype(F32) + got_x[n, :, cols].astype(F32)
        if n < nz - 1:
            mine[n, :, cols] = acc.astype(BF)
            to_z(g, n).start()
        return acc

    def reduce_z(g, acc):
        cols = cols_of(g)
        for n in range(nz - 1):
            to_z(g, n).wait_recv()
            acc = acc + got_z[n, :, cols].astype(F32)
        fin[:, cols] = acc.astype(BF)

    def give(p, to):
        return remote(
            gatt_ref.at[:, pl.ds(al((1 - sq) * half + p * 128), 128)],
            grad.at[p, pl.ds(to, rows)],
            send_g.at[p],
            recv_g.at[p],
            partner,
        )

    for p in range(pairs):
        give(p, base).start()
    start_part(1)
    for p in range(pairs):
        grad[p, pl.ds(base, rows), :] = gatt_ref[:, pl.ds(al(sq * half + p * 128), 128)]
    sums[:, cols_of(1)] = dout_ref[...]
    for n in range(nz):
        for i in range(2):
            to_core(1, n, i).start()
    seg_row, seg_col = eighth(seg_ref[...], prompt)
    gain = w_ref[:, own_cols:lead].astype(F32).T[EXPERTS : EXPERTS + 1, :]

    def norm_of(at):
        xf = xs_ref[at, :].astype(F32)
        r_one = lax.rsqrt(jnp.mean(xf * xf, axis=1, keepdims=True) + EPSILON)
        return xf * r_one, r_one

    for i in range(2):
        at = slice(i * rows, (i + 1) * rows)
        norm_t[:, at] = (norm_of(at)[0] * gain).astype(BF).T

    blocks = 2 * rows // QB
    scale = HEAD_DIM ** (-0.5)
    zero = jnp.zeros((), BF)

    @pl.loop(0, pairs)
    def _(p):
        give(p, there).wait_recv()
        kt[...] = qkv_ref[p, 1].T
        prod = (grad[p].astype(F32) * mixed_ref[p].astype(F32)).T
        delta = []
        for h in range(2):
            lanes = iota((1, 128), 1) // HEAD_DIM == h
            qm[h] = jnp.where(lanes, qkv_ref[p, 0], zero) * jnp.asarray(scale, BF)
            dom[h] = jnp.where(lanes, grad[p], zero)
            low = h * HEAD_DIM
            delta.append(jnp.sum(prod[low : low + HEAD_DIM, :], axis=0, keepdims=True))
        for j in range(blocks):
            keys = slice(j * QB, (j + 1) * QB)
            k, v = qkv_ref[p, 1, keys, :], qkv_ref[p, 2, keys, :]
            dk = dv = None
            for i in range(j, blocks):
                at = slice(i * QB, (i + 1) * QB)
                mask = allowed_tile(j, i, prompt, seg_col, seg_row)
                for h in range(2):
                    s = nt(k, qm[h, at, :])
                    dpr = nt(v, dom[h, at, :])
                    pr = jnp.exp2(s * LOG2E - lse_ref[p, h : h + 1, at])
                    if mask is not None:
                        pr = jnp.where(mask, pr, 0.0)
                    ds = (pr * (dpr - delta[h][:, at])).astype(BF)
                    a = nn(pr.astype(BF), dom[h, at, :])
                    b = nn(ds, qm[h, at, :])
                    c = nn(kt[h * HEAD_DIM : (h + 1) * HEAD_DIM, keys], ds)
                    dv = a if dv is None else dv + a
                    dk = b if dk is None else dk + b
                    to = slice(h * HEAD_DIM, (h + 1) * HEAD_DIM)
                    dqt[to, at] = c if j == 0 else dqt[to, at] + c
            dcat[keys, pl.ds(al(half + p * 128), 128)] = dk.astype(BF)
            dcat[keys, pl.ds(al(2 * half + p * 128), 128)] = dv.astype(BF)
        dcat[:, pl.ds(al(p * 128), 128)] = (dqt[...] * scale).T.astype(BF)

        @pl.when(p == 0)
        def _():
            sum_part(0)
            start_part(2)
            for n in range(nz):
                reduce_core(1, n)

        @pl.when(p == 1)
        def _():
            pass_part(0)
            sum_part(1)
            start_part(3)
            for n in range(nz - 1):
                reduce_x(1, n)

    partial = nt(dcat[pl.ds(there, rows), :], w_ref[:, 0:own_cols])
    send_dx[...] = partial.astype(BF)
    to_dx = remote(send_dx, got_dx, send_d, recv_d, partner)
    to_dx.start()
    dg_one = jnp.sum(partial * norm_of(pl.ds(there, rows))[0], axis=0, keepdims=True)
    partial = nt(dcat[pl.ds(base, rows), :], w_ref[:, 0:own_cols])
    own_gn[...] = partial
    dg_one = dg_one + jnp.sum(partial * norm_of(pl.ds(base, rows))[0], axis=0, keepdims=True)
    stacked = jnp.concatenate([dg_one, dgain_ref[...], jnp.zeros((126, width), F32)], axis=0).T
    lane = iota((1, 128), 1)
    small = jnp.where(lane < EXPERTS, droute_ref[...], 0.0)
    for i in range(2):
        small = jnp.where(lane == EXPERTS + i, stacked[:, i : i + 1], small)
    sums[:, own_cols:lead] = small.astype(BF)
    for n in range(nz):
        zone = pl.ds(pl.multiple_of(order[n] * shard, shard), shard)
        sums[zone, 0:own_cols] = nn(norm_t[zone, :], dcat[...]).astype(BF)
        for i in range(2):
            to_core(0, n, i).start()
    pass_part(1)
    sum_part(2)
    last_part(0)
    reduce_core(0, 0)
    for n in range(1, nz):
        reduce_core(0, n)
        reduce_x(0, n - 1)
    reduce_z(1, reduce_x(1, nz - 1))
    last_part(1)
    pass_part(2)
    sum_part(3)
    reduce_z(0, reduce_x(0, nz - 1))
    to_f = remote(fin, got_f, send_f, recv_f, partner)
    to_f.start()
    to_dx.wait_recv()
    grad_n = own_gn[...] + got_dx[...].astype(F32)
    x_norm, r_one = norm_of(pl.ds(base, rows))
    u = grad_n * gain
    dx = gh_ref[...] + r_one * (u - x_norm * jnp.mean(u * x_norm, axis=1, keepdims=True))
    dx_ref[...] = dx.astype(BF)
    pass_part(3)
    last_part(2)
    to_f.wait_recv()

    def spot(px, co):
        return pl.ds(pl.multiple_of((px * 2 + co) * part, part), part)

    here = spot(x, core)
    for i in range(3):
        cols = slice(i * half, (i + 1) * half)
        total[here, pl.ds(al(i * width + sq * half), half)] = fin[:, cols]
        total[here, pl.ds(al(i * width + (1 - sq) * half), half)] = got_f[:, cols]
    total[here, 3 * width :] = (fin[:, own_cols:].astype(F32) + got_f[:, own_cols:].astype(F32)).astype(BF)

    def pass_on(px, co, send, recv, peer):
        return remote(total.at[spot(px, co)], total.at[spot(px, co)], send, recv, peer)

    pass_on(x, core, send_a, recv_a, across).start()
    pass_on(x, core, send_b.at[0], recv_b.at[0], sibling).start()
    pass_on(1 - x, core, send_a, recv_a, across).wait_recv()
    pass_on(1 - x, core, send_b.at[1], recv_b.at[1], sibling).start()
    pass_on(x, 1 - core, send_b.at[0], recv_b.at[0], sibling).wait_recv()
    pass_on(1 - x, 1 - core, send_b.at[1], recv_b.at[1], sibling).wait_recv()
    din_out[...] = total[:, 0 : 3 * width].astype(F32)
    small = total[:, 3 * width : 3 * width + 128].astype(F32)
    droute_out[...] = small[:, 0:EXPERTS]
    dgains_out[...] = small[:, EXPERTS : EXPERTS + 2]
    dout_out[...] = total[:, 3 * width + 128 :].astype(F32)
    last_part(3)
    for k in range(PARTS):
        end_part(k)
    pass_on(x, core, send_a, recv_a, across).wait_send()
    pass_on(x, core, send_b.at[0], recv_b.at[0], sibling).wait_send()
    pass_on(1 - x, core, send_b.at[1], recv_b.at[1], sibling).wait_send()
    to_f.wait_send()
    to_dx.wait_send()
    for g in range(2):
        for n in range(nz):
            for i in range(2):
                to_core(g, n, i).wait_send()
            to_x(g, n).wait_send()
            if n < nz - 1:
                to_z(g, n).wait_send()
    for p in range(pairs):
        give(p, base).wait_send()


def finish(xs, grad_att, qkv, mixed, lse, whole, grad_hidden, d_out, d_route, d_gain, segments, dw_half, dw_first, prompt, nz, cid):
    rows, width = grad_att.shape
    pairs = width // 256
    cols = whole.shape[1]
    shard = width // nz
    part = shard // 4
    group = 2 * rows
    dma = pltpu.SemaphoreType.DMA
    two = lambda *shape: [dma(shape), dma(shape)]
    vm = pltpu.VMEM
    return pl.pallas_call(
        functools.partial(finish_kernel, prompt, nz),
        out_shape=(
            sds((rows, width), BF),
            sds((shard, 3 * width), F32),
            sds((shard, width), F32),
            sds((shard, EXPERTS), F32),
            sds((shard, 2), F32),
            sds((PARTS - 1,) + dw_first.shape, BF),
            sds((2, 4) + dw_half.shape[1:], BF),
        ),
        in_specs=[VM] * 11 + [ANY, ANY],
        out_specs=(VM,) * 5 + (ANY, ANY),
        scratch_shapes=[
            vm((pairs, group, 128), BF),
            vm((2, group, 128), BF),
            vm((2, group, 128), BF),
            vm((128, group), BF),
            vm((128, group), F32),
            vm((group, 3 * width // 2), BF),
            vm((width, group), BF),
            vm((width, cols), BF),
            vm((nz, 2, part, cols), BF),
            vm((nz, part, cols), BF),
            vm((nz - 1, part, cols), BF),
            vm((nz - 1, part, cols), BF),
            vm((part, cols), BF),
            vm((part, cols), BF),
            vm((shard, 4 * width + 128), BF),
            vm((rows, width), BF),
            vm((rows, width), BF),
            vm((rows, width), F32),
            vm((nz,) + dw_first.shape[1:], BF),
            vm((PARTS,) + dw_first.shape[1:], BF),
            dma((nz + PARTS,)),
        ]
        + two(pairs) + two(2, nz, 2) + two(2, nz) + two(2, nz - 1) + two() + two() + two() + two(2)
        + two(PARTS - 1, nz - 1) + two(PARTS) + two(PARTS, 2) + two(PARTS, 4),
        compiler_params=params(cid),
        name="finish",
    )(xs, grad_att, qkv, mixed, lse, whole, grad_hidden, d_out, d_route, d_gain, segments, dw_half, dw_first)


def spread_kernel(in_ref, out_ref):
    for e in range(EXPERTS):
        out_ref[:, e, :] = in_ref[e].astype(F32)


def spread_experts(parts):
    cores, experts_, r, k = parts.shape
    block = r // 8
    return pl.pallas_call(
        spread_kernel,
        grid=(cores, 8),
        out_shape=sds((cores * r, experts_, k), F32),
        in_specs=[pl.BlockSpec((None, experts_, block, k), lambda c, i: (c, 0, i, 0))],
        out_specs=pl.BlockSpec((block, experts_, k), lambda c, i: (c * 8 + i, 0, 0)),
        compiler_params=params(),
        name="spread",
    )(parts)


def shards(tokens, attn_in, attn_out, router, gains, expert_w, expert_ids, segments, cotangent):
    x = tokens[0]
    cot = cotangent[0]
    rows, width = x.shape
    nz = lax.axis_size("fsdp")
    group = 2 * rows
    prompt = group - segments.shape[1]
    capacity = 2 * rows // EXPERTS
    dp, sq = lax.axis_index("dp"), lax.axis_index("seq")
    core = lax.rem(dp, 2)
    mine = (dp // 2) * 2 + sq

    part = expert_w.shape[0] // 2
    piece = lax.dynamic_slice(expert_w, (core * part, mine, 0), (part, 1, 2 * width))[:, 0]
    xs, whole, qkv, mixed, lse, attended, raw, places_row, places_col, near = begin(
        x, attn_in, attn_out, router, gains, segments, expert_ids[0], cot, piece, prompt, nz, capacity, 0
    )
    hidden, probs, gin, res, inner, dw_half = experts(
        x, attended, whole, places_row, places_col, raw, near, capacity, nz, 1
    )
    block_out, grad_hidden, grad_att, d_out, d_route, d_gain_two, dw_first = after(
        gin, res, inner, hidden, probs, places_col, cot, whole, attended, dw_half, capacity, 2
    )
    d_tokens, d_in, d_out, d_route, d_gains, _, dw_all = finish(
        xs, grad_att, qkv, mixed, lse, whole, grad_hidden, d_out, d_route, d_gain_two, segments, dw_half, dw_first,
        prompt, nz, 3,
    )
    d_expert = spread_experts(dw_all)
    return (
        block_out[None],
        d_tokens[None],
        d_in,
        d_out,
        d_route,
        d_gains,
        d_expert,
    )


def route(choose, capacity, experts_count):
    pair_expert = choose.reshape(-1)
    one_hot = (pair_expert[:, None] == jnp.arange(experts_count, dtype=jnp.int32)[None, :]).astype(
        jnp.int32
    )
    before = jnp.cumsum(one_hot, axis=0) - one_hot
    place = jnp.sum(before * one_hot, axis=1)
    kept = place < capacity
    slots = jnp.where(kept, pair_expert * capacity + place, experts_count * capacity)
    pair_count = pair_expert.shape[0]
    pair_of = (
        jnp.zeros((experts_count * capacity + 1,), jnp.int32)
        .at[slots]
        .set(jnp.arange(pair_count, dtype=jnp.int32))
    )
    filled = (
        jnp.zeros((experts_count * capacity + 1,), jnp.int32)
        .at[slots]
        .set(jnp.ones((pair_count,), jnp.int32))
    )
    return (slots, kept, pair_of[:-1], filled[:-1] > 0)


def expert_pre(expert_in, piece):
    width = piece.shape[2] // 2
    return jnp.einsum(
        "ecd,fed->ecf", expert_in, piece[:, :, :width], preferred_element_type=jnp.float32
    )


def expert_out(activity, piece):
    width = piece.shape[2] // 2
    return jnp.einsum(
        "ecf,fed->ecd", activity, piece[:, :, width:], preferred_element_type=jnp.float32
    )


def expert_back(grad_result, pre_rows, piece):
    width = piece.shape[2] // 2
    grad_act = jnp.einsum(
        "ecd,fed->ecf", grad_result, piece[:, :, width:], preferred_element_type=jnp.float32
    )
    grad_pre = jax.vjp(jax.nn.gelu, pre_rows)[1](grad_act)[0].astype(jnp.bfloat16)
    grad_in = jnp.einsum(
        "ecf,fed->ecd", grad_pre, piece[:, :, :width], preferred_element_type=jnp.float32
    )
    return (grad_pre, grad_in)


def general_shards(tokens, attn_in, attn_out, router, gains, expert_w, expert_ids, segments, cotangent):
    x_rows = tokens[0].astype(jnp.float32)
    tok_rows = x_rows.shape[0]
    width = x_rows.shape[1]
    seq_count = lax.axis_size("seq")
    scale = HEAD_DIM ** (-0.5)
    w_qkv, w_proj, w_route, gain_pair = (
        lax.all_gather(attn_in, "fsdp", axis=0, tiled=True),
        lax.all_gather(attn_out, "fsdp", axis=0, tiled=True),
        lax.all_gather(router, "fsdp", axis=0, tiled=True),
        lax.all_gather(gains, "fsdp", axis=0, tiled=True),
    )
    gain_f = gain_pair.astype(jnp.float32)
    r_one = lax.rsqrt(jnp.mean(x_rows * x_rows, axis=-1, keepdims=True) + EPSILON)
    normed_one = x_rows * r_one
    normed_low = (normed_one * gain_f[:, 0]).astype(jnp.bfloat16)
    projected = jnp.dot(normed_low, w_qkv, preferred_element_type=jnp.float32).astype(jnp.bfloat16)
    local_heads = HEADS // seq_count
    head_cols = local_heads * HEAD_DIM
    arrived = lax.all_to_all(
        projected.reshape(tok_rows, 3, seq_count, head_cols),
        "seq",
        split_axis=2,
        concat_axis=0,
        tiled=True,
    )
    group_len = arrived.shape[0]
    queries = arrived[:, 0, 0].reshape(group_len, local_heads, HEAD_DIM)
    keys = arrived[:, 1, 0].reshape(group_len, local_heads, HEAD_DIM)
    values = arrived[:, 2, 0].reshape(group_len, local_heads, HEAD_DIM)
    seg_full = jnp.concatenate([jnp.full((PROMPT,), -1, jnp.int32), segments[0]])
    block = min(512, group_len)
    key_place = jnp.arange(group_len, dtype=jnp.int32)
    begins = jnp.arange(group_len // block, dtype=jnp.int32) * block

    def block_scores(begin):
        query_block = lax.dynamic_slice_in_dim(queries, begin, block, 0)
        query_place = begin + jnp.arange(block, dtype=jnp.int32)
        query_seg = lax.dynamic_slice_in_dim(seg_full, begin, block, 0)
        raw = (
            jnp.einsum("qhd,khd->hqk", query_block, keys, preferred_element_type=jnp.float32)
            * scale
        )
        allowed = (key_place[None, :] <= query_place[:, None]) & (
            (seg_full[None, :] < 0) | (seg_full[None, :] == query_seg[:, None])
        )
        return (jnp.where(allowed[None], raw, NEGATIVE), query_block)

    def forward_block(begin):
        masked, query_block = block_scores(begin)
        row_max = jnp.max(masked, axis=-1, keepdims=True)
        expo = jnp.exp(masked - row_max)
        row_total = jnp.sum(expo, axis=-1, keepdims=True)
        probs = expo / row_total
        mixed_block = jnp.einsum(
            "hqk,khd->qhd", probs.astype(jnp.bfloat16), values, preferred_element_type=jnp.float32
        )
        return (mixed_block.astype(jnp.bfloat16), (row_max + jnp.log(row_total))[:, :, 0])

    mixed_blocks, log_totals = lax.map(forward_block, begins)
    mixed_heads = mixed_blocks.reshape(group_len, 1, head_cols)
    returned = lax.all_to_all(mixed_heads, "seq", split_axis=0, concat_axis=1, tiled=True)
    attended = returned.reshape(tok_rows, width)
    hidden = x_rows + jnp.dot(attended, w_proj, preferred_element_type=jnp.float32)
    r_two = lax.rsqrt(jnp.mean(hidden * hidden, axis=-1, keepdims=True) + EPSILON)
    normed_two = hidden * r_two
    routed_low = (normed_two * gain_f[:, 1]).astype(jnp.bfloat16)
    logits = jnp.dot(routed_low, w_route, preferred_element_type=jnp.float32)
    probs_r = jax.nn.softmax(logits, axis=-1)
    choose = expert_ids[0]
    choose_map = (choose[:, :, None] == jnp.arange(EXPERTS, dtype=jnp.int32)[None, None, :]).astype(
        jnp.float32
    )
    gates = jnp.sum(probs_r[:, None, :] * choose_map, axis=-1)
    capacity = 2 * tok_rows // EXPERTS
    slots, kept, pair_of, filled = route(choose, capacity, EXPERTS)
    token_of = pair_of // 2
    expert_in = jnp.where(
        filled[:, None], routed_low[token_of], jnp.zeros((), jnp.bfloat16)
    ).reshape(EXPERTS, capacity, width)
    piece = lax.all_gather(expert_w, "fsdp", axis=0, tiled=True)
    pre_rows = expert_pre(expert_in, piece)
    result = expert_out(jax.nn.gelu(pre_rows).astype(jnp.bfloat16), piece)
    padded = jnp.concatenate(
        [result.reshape(EXPERTS * capacity, width), jnp.zeros((1, width), jnp.float32)], axis=0
    )
    picked = padded[slots].reshape(tok_rows, 2, width)
    kept_f = kept.astype(jnp.float32).reshape(tok_rows, 2)
    weight_pair = gates * kept_f
    block_out = hidden + jnp.sum(weight_pair[..., None] * picked, axis=1)
    grad_out_rows = cotangent[0].astype(jnp.float32)
    grad_gates = kept_f * jnp.sum(grad_out_rows[:, None, :] * picked, axis=-1)
    grad_probs = jnp.sum(grad_gates[:, :, None] * choose_map, axis=1)
    grad_logits = probs_r * (grad_probs - jnp.sum(probs_r * grad_probs, axis=-1, keepdims=True))
    grad_route_w = jnp.dot(routed_low.astype(jnp.float32).T, grad_logits, precision=HIGH)
    grad_routed = jnp.dot(grad_logits, w_route.astype(jnp.float32).T, precision=HIGH)
    scaled = (weight_pair[:, :, None] * grad_out_rows[:, None, :]).reshape(2 * tok_rows, width)
    grad_result = (
        jnp.where(filled[:, None], scaled[pair_of], 0.0)
        .astype(jnp.bfloat16)
        .reshape(EXPERTS, capacity, width)
    )
    piece = lax.all_gather(expert_w, "fsdp", axis=0, tiled=True)
    pre_rows = expert_pre(expert_in, piece)
    act_rows = jax.nn.gelu(pre_rows).astype(jnp.bfloat16)
    grad_pre_rows, grad_in_rows = expert_back(grad_result, pre_rows, piece)
    act_store = act_rows
    pre_rows = grad_pre_rows
    act_rows = act_store
    grad_first = jnp.einsum("ecd,ecf->fed", expert_in, pre_rows, preferred_element_type=jnp.float32)
    grad_second = jnp.einsum(
        "ecf,ecd->fed", act_rows, grad_result, preferred_element_type=jnp.float32
    )
    expert_shard = lax.psum_scatter(
        jnp.concatenate([grad_first, grad_second], axis=2).astype(jnp.bfloat16),
        "fsdp",
        scatter_dimension=0,
        tiled=True,
    )
    padded_in = jnp.concatenate(
        [grad_in_rows.reshape(EXPERTS * capacity, width), jnp.zeros((1, width), jnp.float32)],
        axis=0,
    )
    grad_routed = grad_routed + jnp.sum(padded_in[slots].reshape(tok_rows, 2, width), axis=1)
    grad_gain_two = jnp.sum(grad_routed * normed_two, axis=0)
    scaled_two = grad_routed * gain_f[:, 1]
    grad_hidden = grad_out_rows + r_two * (
        scaled_two - normed_two * jnp.mean(scaled_two * normed_two, axis=-1, keepdims=True)
    )
    hid_low = grad_hidden.astype(jnp.bfloat16)
    grad_proj_w = jnp.dot(attended.T, hid_low, preferred_element_type=jnp.float32)
    grad_attended = jnp.dot(hid_low, w_proj.T, preferred_element_type=jnp.float32).astype(
        jnp.bfloat16
    )
    grad_heads = lax.all_to_all(
        grad_attended.reshape(tok_rows, seq_count, head_cols),
        "seq",
        split_axis=1,
        concat_axis=0,
        tiled=True,
    )
    grad_mixed = grad_heads.reshape(group_len, local_heads, HEAD_DIM)

    def back_block(carry, inputs):
        begin, log_rows = inputs
        masked, query_block = block_scores(begin)
        probs = jnp.exp(masked - log_rows[:, :, None])
        grad_block = lax.dynamic_slice_in_dim(grad_mixed, begin, block, 0)
        grad_p = jnp.einsum("qhd,khd->hqk", grad_block, values, preferred_element_type=jnp.float32)
        inner = jnp.sum(probs * grad_p, axis=-1, keepdims=True)
        grad_scores = (probs * (grad_p - inner)).astype(jnp.bfloat16)
        grad_query = (
            jnp.einsum("hqk,khd->qhd", grad_scores, keys, preferred_element_type=jnp.float32)
            * scale
        )
        grad_key = (
            carry[0]
            + jnp.einsum(
                "hqk,qhd->khd", grad_scores, query_block, preferred_element_type=jnp.float32
            )
            * scale
        )
        grad_value = carry[1] + jnp.einsum(
            "hqk,qhd->khd",
            probs.astype(jnp.bfloat16),
            grad_block,
            preferred_element_type=jnp.float32,
        )
        return ((grad_key, grad_value), grad_query)

    zero_heads = jnp.zeros((group_len, local_heads, HEAD_DIM), jnp.float32)
    (grad_keys, grad_values), grad_queries = lax.scan(
        back_block, (zero_heads, zero_heads), (begins, log_totals)
    )
    stacked = jnp.stack(
        [
            grad_queries.reshape(group_len, head_cols),
            grad_keys.reshape(group_len, head_cols),
            grad_values.reshape(group_len, head_cols),
        ],
        axis=1,
    )
    stacked = stacked.astype(jnp.bfloat16).reshape(group_len, 3, 1, head_cols)
    grad_back = lax.all_to_all(stacked, "seq", split_axis=0, concat_axis=2, tiled=True)
    grad_proj_rows = grad_back.reshape(tok_rows, 3 * width)
    grad_qkv_w = jnp.dot(normed_low.T, grad_proj_rows, preferred_element_type=jnp.float32)
    grad_normed = jnp.dot(grad_proj_rows, w_qkv.T, preferred_element_type=jnp.float32)
    grad_gain_one = jnp.sum(grad_normed * normed_one, axis=0)
    scaled_one = grad_normed * gain_f[:, 0]
    grad_x = grad_hidden + r_one * (
        scaled_one - normed_one * jnp.mean(scaled_one * normed_one, axis=-1, keepdims=True)
    )
    grad_gains = jnp.stack([grad_gain_one, grad_gain_two], axis=1)
    shard_qkv, shard_proj, shard_route, shard_gains = (
        lax.psum_scatter(
            grad_qkv_w.astype(jnp.bfloat16), "fsdp", scatter_dimension=0, tiled=True
        ).astype(jnp.float32),
        lax.psum_scatter(
            grad_proj_w.astype(jnp.bfloat16), "fsdp", scatter_dimension=0, tiled=True
        ).astype(jnp.float32),
        lax.psum_scatter(
            grad_route_w.astype(jnp.bfloat16), "fsdp", scatter_dimension=0, tiled=True
        ).astype(jnp.float32),
        lax.psum_scatter(
            grad_gains.astype(jnp.bfloat16), "fsdp", scatter_dimension=0, tiled=True
        ).astype(jnp.float32),
    )
    part_qkv, part_proj, part_expert = (
        lax.psum_scatter(
            shard_qkv.astype(jnp.bfloat16), ("dp", "seq"), scatter_dimension=1, tiled=True
        ).astype(jnp.float32),
        lax.psum_scatter(
            shard_proj.astype(jnp.bfloat16), ("dp", "seq"), scatter_dimension=1, tiled=True
        ).astype(jnp.float32),
        lax.psum_scatter(expert_shard, ("dp", "seq"), scatter_dimension=2, tiled=True).astype(
            jnp.float32
        ),
    )
    summed_qkv, summed_proj, summed_expert = (
        lax.all_gather(part_qkv.astype(jnp.bfloat16), ("dp", "seq"), axis=1, tiled=True).astype(
            part_qkv.dtype
        ),
        lax.all_gather(part_proj.astype(jnp.bfloat16), ("dp", "seq"), axis=1, tiled=True).astype(
            part_proj.dtype
        ),
        lax.all_gather(part_expert.astype(jnp.bfloat16), ("dp", "seq"), axis=2, tiled=True).astype(
            part_expert.dtype
        ),
    )
    summed_route, summed_gains = lax.psum((shard_route, shard_gains), ("dp", "seq"))
    return (
        block_out.astype(jnp.bfloat16)[None],
        grad_x.astype(jnp.bfloat16)[None],
        summed_qkv,
        summed_proj,
        summed_route,
        summed_gains,
        summed_expert,
    )


def fits(mesh):
    return mesh.shape["fsdp"] == 4 and mesh.shape["dp"] == 4 and mesh.shape["seq"] == 2


def solution(mesh):
    body = shards if fits(mesh) else general_shards
    in_specs = (
        P(("dp", "fsdp"), "seq", None),
        P("fsdp", None),
        P("fsdp", None),
        P("fsdp", None),
        P("fsdp", None),
        P("fsdp", None, None),
        P(("dp", "fsdp"), "seq", None),
        P(("dp", "fsdp"), None),
        P(("dp", "fsdp"), "seq", None),
    )
    out_specs = (
        P(("dp", "fsdp"), "seq", None),
        P(("dp", "fsdp"), "seq", None),
        P("fsdp", None),
        P("fsdp", None),
        P("fsdp", None),
        P("fsdp", None),
        P("fsdp", None, None),
    )
    return jax.shard_map(body, mesh=mesh, in_specs=in_specs, out_specs=out_specs, check_vma=False)
```

profile of v0, /device:TPU:9, one launch (start us, length us, event | category | flops | bytes accessed | tf_op | source)
XLA Modules:
  0.0 400.1 jit_solution(10604086662749600109)
XLA Ops:
  0.7 1.4 copy.23.router_ref
  2.1 1.4 copy.24.gains_ref
  3.5 1.6 copy.21
  5.1 4.8 %constant_dynamic-slice_fusion = bf16[384,1,1536]{2,1,0:T(2,128)(2,1)S(1)} fusion(bf16[768,4,1536]{2,1,0:T(4,128)(2,1)} %param.14, s32[]{:T(128)S(6)} %select_n.11, s32[]{:T(128)S(6)} %select_n.13), kind=kLoop, calls=%fused_computation.1 | loop fusion | bytes 2359304 | tf_op jit(solution)/shard_map/dynamic_slice | solution.py:1166
  9.9 1.2 copy.29
  11.1 76.2 %begin.1 = (bf16[1536,768]{1,0:T(8,128)(2,1)}, bf16[768,2048]{1,0:T(8,128)(2,1)}, bf16[3,3,1536,128]{3,2,1,0:T(8,128)(2,1)}, bf16[3,1536,128]{2,1,0:T(8,128)(2,1...) custom-call(bf16[768,768]{1,0:T(8,128)(2,1)} %bitcast.11, ...), custom_call_target="tpu_custom_call" | custom-call | tf_op jit(solution)/shard_map/begin/pallas_call | solution.py:348
  87.3 99.3 %experts.1 = (f32[768,768]{1,0:T(8,128)}, f32[768,128]{1,0:T(8,128)}, bf16[4,384,768]{2,1,0:T(8,128)(2,1)}, bf16[4,384,768]{2,1,0:T(8,128)(2,1)}, f32[4,8,384]{2,1,0:T(8,128)}, /*index=5*/bf16[4,384,1536]{2,1,0:T(8,128)(2,1)}) custom-call(bf16[768,768]{1,0:T(8,128)(2,1)} %bitcast.12, bf16[768,768]{1,0:T(8,128)(2,1)} %get-tuple-element.36.att_ref, ...), custom_call_target="tpu_custom_call" | custom-call | tf_op jit(solution)/shard_map/experts/pallas_call | solution.py:625
  186.6 58.2 %after.1 = (bf16[768,768]{1,0:T(8,128)(2,1)}, f32[768,768]{1,0:T(8,128)}, bf16[768,768]{1,0:T(8,128)(2,1)}, bf16[768,768]{1,0:T(8,128)(2,1)}, f32[768,128]{1,0:T...) custom-call(bf16[4,384,768]{2,1,0:T(8,128)(2,1)} %get-tuple-element.42.gin_ref, ...), custom_call_target="tpu_custom_call" | custom-call | tf_op jit(solution)/shard_map/after/pallas_call | solution.py:733
  244.9 131.7 %finish.1 = (bf16[768,768]{1,0:T(8,128)(2,1)}, f32[192,2304]{1,0:T(8,128)}, f32[192,768]{1,0:T(8,128)}, f32[192,4]{1,0:T(8,128)}, f32[192,2]{1,0:T(8,128)}, /*in...) custom-call(bf16[1536,768]{1,0:T(8,128)(2,1)} %get-tuple-element.49.xs_ref, ...), custom_call_target="tpu_custom_call" | custom-call | tf_op jit(solution)/shard_map/finish/pallas_call | solution.py:1091
  376.6 1.6 copy.26
  378.1 1.6 copy.25
  379.7 0.0 copy-start.1
  379.7 0.0 copy-start.2
  379.7 15.8 %spread.1 = f32[768,4,1536]{2,1,0:T(4,128)} custom-call(bf16[2,4,384,1536]{3,2,1,0:T(8,128)(2,1)} %get-tuple-element.64.in_ref), custom_call_target="tpu_custom_call" | custom-call | tf_op jit(solution)/shard_map/spread/pallas_call | solution.py:1142
  395.5 0.0 copy-done.1
  395.5 0.0 copy-start
  395.5 1.0 copy.34
  396.5 0.0 copy-done.2
  396.5 1.0 copy.35
  397.5 0.0 copy-done
  397.5 0.0 copy-start.3
  397.5 1.2 copy.36
  398.8 0.3 copy-done.3
  399.0 0.8 copy.37
Async XLA Ops:
  379.7 15.8 %copy-start.1 = (bf16[768,768]{1,0:T(8,128)(2,1)S(1)}, bf16[768,768]{1,0:T(8,128)(2,1)}, u32[]{:S(2)}) copy-start(bf16[768,768]{1,0:T(8,128)(2,1)} %get-tuple-element.48) | copy-start | bytes 3538948
  379.7 16.8 %copy-start.2 = (bf16[768,768]{1,0:T(8,128)(2,1)S(1)}, bf16[768,768]{1,0:T(8,128)(2,1)}, u32[]{:S(2)}) copy-start(bf16[768,768]{1,0:T(8,128)(2,1)} %get-tuple-element.59) | copy-start | bytes 3538948
  395.5 2.0 copy-start
  397.5 1.5 copy-start.3
where the time goes:
time: 405 us; the launch traced here: 400 us
  Pallas kernels  381 us (94%)
  local copies, waits for them, and re-layouts  17.8 us (4%)
    pallas_call x1, Pallas kernels, finish(): pl.pallas_call(functools.partial(finish_kernel, prompt, nz), out_shape=(s...  132 us
    pallas_call x1, Pallas kernels, experts(): pl.pallas_call(functools.partial(experts_kernel, capacity, nz), out_shape...  99.3 us
    pallas_call x1, Pallas kernels, begin(): pl.pallas_call(functools.partial(begin_kernel, prompt, nz, capacity), out...  76.2 us
    pallas_call x1, Pallas kernels, after(): pl.pallas_call(functools.partial(after_kernel, capacity, nz), out_shape=(...  58.2 us
    pallas_call x1, Pallas kernels, spread_experts(): pl.pallas_call(spread_kernel, grid=(cores, 8), out_shape=sds((cores * r,...  15.8 us
    unnamed x18, local copies, waits for them, and re-layouts  13.1 us

commit v1 on v0

--- a/solution.py
+++ b/solution.py
@@ -425,13 +425,22 @@
     corner = [flip_chip(x, sq, *f) for f in SOURCES]
     plane = [(px * 2 + core, py, z) for px, py in corner]
     experts_of = [px * 2 + py for px, py in corner]
-    below, above = (dp, sq, lax.rem(z + nz - 1, nz)), (dp, sq, lax.rem(z + 1, nz))
+    beside_z = (dp, sq, z + 1 - 2 * lax.rem(z, 2))
     shift = jnp.where(z >= nz // 2, 1, 0)
     far_zone = jnp.where(z >= nz // 2, 0, nz - 1)
-    greet([sibling, below, above] + [plane[j] for j in AWAY])
+    at_end = (z == 0) | (z == nz - 1)
+    near_peers = [sibling] + [plane[j] for j in AWAY]
+    barrier = pltpu.get_barrier_semaphore()
+    for peer in near_peers:
+        pl.semaphore_signal(barrier, inc=1, device_id=peer, device_id_type=MESH)
+
+    @pl.when(at_end)
+    def _():
+        pl.semaphore_signal(barrier, inc=1, device_id=beside_z, device_id_type=MESH)
+
+    pl.semaphore_wait(barrier, len(near_peers) + jnp.where(at_end, 0, 1))
     line = Line(nz, dp, sq, z, lambda stage, zone: near_ref.at[zone], own_w, line_sems)
     line.start(nz - 1)
-    at_end = (z == 0) | (z == nz - 1)
 
     def go_raw(j):
         return remote(raw_send.at[j], raw_ref.at[j], send_x.at[j], recv_x.at[j], plane[j])
@@ -658,119 +667,20 @@
     )(x, attended, whole, places_row, places_col, raw, near)
 
 
-def after_kernel(
-    capacity, nz, gin_ref, res_ref, dot_ref, hidden_ref, probs_ref, places_col, cot_ref, w_hbm, att_ref, part_ref,
-    out_ref, gh_ref, gatt_ref, dw_ref, dr_ref, dg_ref, got_ref,
-    wp, got_res, local, send, recv, send_z, recv_z,
+PARTS = 4
+
+
+def finish_kernel(
+    prompt, nz, capacity, xs_ref, qkv_ref, mixed_ref, lse_ref, w_ref, seg_ref, hidden_ref, probs_ref, places_ref,
+    dot_ref, gin_ref, res_ref, cot_ref, att_ref, part_ref,
+    out_ref, dx_ref, din_out, dout_out, droute_out, dgains_out, got_up, got_down, dw_all,
+    gh, gatt, got_res, grad, qm, dom, kt, dqt, dcat, norm_t, sums, got_c, got_x, got_z, mine, fin, got_f, total,
+    send_dx, got_dx, own_gn, stage, dw_sum, ahead,
+    local, send_r, recv_r, send_g, recv_g, send_c, recv_c, send_x, recv_x, send_z, recv_z, send_d, recv_d, send_f, recv_f,
+    send_a, recv_a, send_b, recv_b, send_u, recv_u, send_l, recv_l, send_v, recv_v, send_h, recv_h, send_k, recv_k,
 ):
     dp, sq, z, x, core = place()
-    rows, width = hidden_ref.shape
-    corner = [flip_chip(x, sq, *f) for f in SOURCES]
-    plane = [(px * 2 + core, py, z) for px, py in corner]
-    experts_of = [px * 2 + py for px, py in corner]
-    others = [(dp, sq, lax.rem(z + d, nz)) for d in range(1, nz)]
-    greet([plane[j] for j in AWAY] + others)
-    first = pl.ds(0, got_ref.shape[1])
-    zones = [
-        remote(part_ref.at[lax.rem(z + d, nz), first], got_ref.at[d - 1], send_z.at[d - 1], recv_z.at[d - 1], others[d - 1])
-        for d in range(1, nz)
-    ]
-    for c in zones:
-        c.start()
-    copies = {j: remote(res_ref.at[j], got_res.at[j], send.at[j], recv.at[j], plane[j]) for j in AWAY}
-    for c in copies.values():
-        c.start()
-    load = pltpu.make_async_copy(w_hbm.at[:, 3 * width // 2 :], wp, local)
-    load.start()
-    load.wait()
-    hidden = hidden_ref[...]
-    probs = probs_ref[...]
-    small = wp[:, :128]
-    gain = small.astype(F32).T[EXPERTS + 1 : EXPERTS + 2, :]
-    lane = iota(probs.shape, 1)
-    back = None
-    grad_probs = jnp.zeros_like(probs)
-    for j in range(4):
-        pick = hot_cols(pick_col(places_col[...], experts_of[j]), capacity)
-        part = nn(pick, gin_ref[j])
-        back = part if back is None else back + part
-        inner = jnp.sum(pick.astype(F32) * dot_ref[j][0:1, :], axis=1, keepdims=True)
-        grad_probs = jnp.where(lane == experts_of[j], inner, grad_probs)
-    mixed = jnp.sum(probs * grad_probs, axis=1, keepdims=True)
-    low = (probs * (grad_probs - mixed)).astype(BF)
-    r_two = lax.rsqrt(jnp.mean(hidden * hidden, axis=1, keepdims=True) + EPSILON)
-    h_norm = hidden * r_two
-    routed = (h_norm * gain).astype(BF)
-    grad_routed = back + nt(low, small)
-    dg_ref[...] = jnp.sum(grad_routed * h_norm, axis=0, keepdims=True)
-    u = grad_routed * gain
-    grad_hidden = cot_ref[...].astype(F32) + r_two * (
-        u - h_norm * jnp.mean(u * h_norm, axis=1, keepdims=True)
-    )
-    gh_ref[...] = grad_hidden
-    hid_low = grad_hidden.astype(BF)
-    gatt_ref[...] = nt(hid_low, wp[:, 128:]).astype(BF)
-    dr_ref[...] = tn(routed, low)
-    dw_ref[...] = tn(att_ref[...], hid_low).astype(BF)
-    total = hidden
-    for j in (OWN,) + AWAY:
-        if j != OWN:
-            copies[j].wait_recv()
-        value = res_ref[j] if j == OWN else got_res[j]
-        pick = hot_cols(pick_col(places_col[...], experts_of[j]), capacity)
-        total = total + pick_col(probs, experts_of[j]) * nn(pick, value)
-    out_ref[...] = total.astype(BF)
-    for c in copies.values():
-        c.wait_send()
-    for c in zones:
-        c.wait()
-
-
-def after(gin, res, inner, hidden, probs, places_col, cot, whole, attended, dw_half, capacity, cid):
-    nz, part, deep = dw_half.shape
-    rows, width = hidden.shape
-    dma = pltpu.SemaphoreType.DMA
-    return pl.pallas_call(
-        functools.partial(after_kernel, capacity, nz),
-        out_shape=(
-            sds((rows, width), BF),
-            sds((rows, width), F32),
-            sds((rows, width), BF),
-            sds((width, width), BF),
-            sds((width, 128), F32),
-            sds((1, width), F32),
-            sds((nz - 1, part // PARTS, deep), BF),
-        ),
-        in_specs=[VM] * 7 + [ANY, VM, ANY],
-        out_specs=(VM,) * 6 + (ANY,),
-        scratch_shapes=[
-            pltpu.VMEM((rows, width + 128), BF),
-            pltpu.VMEM((4, capacity, width), BF),
-            dma(()),
-            dma((4,)),
-            dma((4,)),
-            dma((nz - 1,)),
-            dma((nz - 1,)),
-        ],
-        compiler_params=params(cid),
-        name="after",
-    )(gin, res, inner, hidden, probs, places_col, cot, whole, attended, dw_half)
-
-
-PARTS = 4
-
-
-def finish_kernel(
-    prompt, nz, xs_ref, gatt_ref, qkv_ref, mixed_ref, lse_ref, w_ref, gh_ref, dout_ref, droute_ref, dgain_ref,
-    seg_ref, part_ref, got_first,
-    dx_ref, din_out, dout_out, droute_out, dgains_out, got_rest, dw_all,
-    grad, qm, dom, kt, dqt, dcat, norm_t, sums, got_c, got_x, got_z, mine, fin, got_f, total, send_dx, got_dx, own_gn,
-    stage, dw_sum,
-    local, send_g, recv_g, send_c, recv_c, send_x, recv_x, send_z, recv_z, send_d, recv_d, send_f, recv_f,
-    send_a, recv_a, send_b, recv_b, send_s, recv_s, send_v, recv_v, send_h, recv_h, send_k, recv_k,
-):
-    dp, sq, z, x, core = place()
-    rows, width = gatt_ref.shape
+    rows, width = gatt.shape
     half = width // 2
     pairs = half // 128
     shard = width // nz
@@ -785,18 +695,62 @@
     others = [(dp, sq, lax.rem(z + d, nz)) for d in range(1, nz)]
     base = pl.multiple_of(sq * rows, rows)
     there = pl.multiple_of((1 - sq) * rows, rows)
-    greet([sibling, partner, across] + others)
-
-    quarter = got_first.shape[1]
-
-    def zone_part(k, d):
-        return remote(
-            part_ref.at[lax.rem(z + d, nz), pl.ds(k * quarter, quarter)],
-            got_rest.at[k - 1, d - 1],
-            send_s.at[k - 1, d - 1],
-            recv_s.at[k - 1, d - 1],
-            others[d - 1],
-        )
+    corner = [flip_chip(x, sq, *f) for f in SOURCES]
+    plane = [(px * 2 + core, py, z) for px, py in corner]
+    experts_of = [px * 2 + py for px, py in corner]
+    greet([sibling] + [plane[j] for j in AWAY] + others)
+
+    quarter = stage.shape[1]
+
+    def rows_of(k):
+        return pl.ds(k * quarter, quarter)
+
+    def hop(k, t, up, src):
+        to = lax.rem(z + 1, nz) if up else lax.rem(z + nz - 1, nz)
+        got, send, recv = (got_up, send_u, recv_u) if up else (got_down, send_l, recv_l)
+        return remote(src, got.at[k, t], send.at[k, t], recv.at[k, t], (dp, sq, to))
+
+    def legs(slot):
+        ups = (True, slot, list(range(nz - 1, slot, -1)))
+        downs = (False, nz - 1 - slot, list(range(0, nz - 1 - slot)))
+        return ups, downs
+
+    def line_slot(k, slot):
+        for up, sender, zones in legs(slot):
+
+            @pl.when(z == sender)
+            def _(up=up, zones=zones):
+                if slot == 0:
+                    for t in zones:
+                        hop(k, t, up, part_ref.at[t, rows_of(k)]).start()
+                    return
+                got = got_up if up else got_down
+                loads = []
+                for i, t in enumerate(zones):
+                    hop(k, t, up, ahead.at[k % 2, 0]).wait_recv()
+                    loads.append(pltpu.make_async_copy(got.at[k, t], stage.at[2 * i], local.at[2 * i]))
+                    loads.append(pltpu.make_async_copy(part_ref.at[t, rows_of(k)], stage.at[2 * i + 1], local.at[2 * i + 1]))
+                for c in loads:
+                    c.start()
+                for i, t in enumerate(zones):
+                    to = ahead.at[k % 2, i if slot == 1 else 2]
+                    if k > 1:
+                        hop(k - 2, t, up, to).wait_send()
+                    loads[2 * i].wait()
+                    loads[2 * i + 1].wait()
+                    to[...] = (stage[2 * i].astype(F32) + stage[2 * i + 1].astype(F32)).astype(BF)
+                    hop(k, t, up, to).start()
+
+    def line_end():
+        for slot in range(nz - 1):
+            for up, sender, zones in legs(slot):
+
+                @pl.when(z == sender)
+                def _(up=up, zones=zones, slot=slot):
+                    for k in range(PARTS) if slot == 0 else range(PARTS - 2, PARTS):
+                        for i, t in enumerate(zones):
+                            src = part_ref.at[t, rows_of(k)] if slot == 0 else ahead.at[k % 2, i if slot == 1 else 2]
+                            hop(k, t, up, src).wait_send()
 
     def share(k, ch, send, recv, peer, own=False):
         at = dw_all.at[core, ch, pl.ds(k * quarter, quarter)]
@@ -807,28 +761,26 @@
             dw_sum.at[k], dw_all.at[core, chip, pl.ds(k * quarter, quarter)], local.at[nz + k]
         )
 
-    def start_part(k):
-        for d in range(1, nz):
-            zone_part(k, d).start()
-
     def sum_part(k):
-        loads = []
-        for d in range(nz - 1):
-            if k > 0:
-                zone_part(k, d + 1).wait_recv()
-            src = got_first.at[d] if k == 0 else got_rest.at[k - 1, d]
-            loads.append(pltpu.make_async_copy(src, stage.at[d], local.at[d]))
-        loads.append(
-            pltpu.make_async_copy(part_ref.at[z, pl.ds(k * quarter, quarter)], stage.at[nz - 1], local.at[nz - 1])
-        )
-        for c in loads:
-            c.start()
-        for c in loads:
-            c.wait()
-        acc = stage[0].astype(F32)
-        for d in range(1, nz):
-            acc = acc + stage[d].astype(F32)
-        dw_sum[k] = acc.astype(BF)
+        own = pltpu.make_async_copy(part_ref.at[z, rows_of(k)], stage.at[2], local.at[2])
+        own.start()
+        for i, up in enumerate((True, False)):
+            got = got_up if up else got_down
+            has = z > 0 if up else z < nz - 1
+
+            @pl.when(has)
+            def _(i=i, up=up, got=got):
+                hop(k, z, up, ahead.at[0, 0]).wait_recv()
+                c = pltpu.make_async_copy(got.at[k, z], stage.at[i], local.at[i])
+                c.start()
+                c.wait()
+
+            @pl.when(jnp.logical_not(has))
+            def _(i=i):
+                stage[i] = jnp.zeros(stage.shape[1:], BF)
+
+        own.wait()
+        dw_sum[k] = (stage[0].astype(F32) + stage[1].astype(F32) + stage[2].astype(F32)).astype(BF)
         share(k, chip, send_v.at[k], recv_v.at[k], partner, True).start()
         share(k, chip, send_h.at[k, 0], recv_h.at[k, 0], across, True).start()
         share(k, chip, send_k.at[k, 0], recv_k.at[k, 0], sibling, True).start()
@@ -845,19 +797,19 @@
         share(k, chip_d, send_h.at[k, 1], recv_h.at[k, 1], across).wait_recv()
         share(k, chip_d, send_k.at[k, 3], recv_k.at[k, 3], sibling).start()
 
-    def end_part(k):
-        other = [chip, chip_y, chip_x, chip_d]
-        for i in range(4):
-            at = dw_all.at[1 - core, other[i], pl.ds(k * quarter, quarter)]
-            remote(at, at, send_k.at[k, i], recv_k.at[k, i], sibling).wait_recv()
-            share(k, other[i], send_k.at[k, i], recv_k.at[k, i], sibling, i == 0).wait_send()
-        share(k, chip, send_v.at[k], recv_v.at[k], partner, True).wait_send()
-        share(k, chip, send_h.at[k, 0], recv_h.at[k, 0], across, True).wait_send()
-        share(k, chip_y, send_h.at[k, 1], recv_h.at[k, 1], across).wait_send()
-        keep(k).wait()
-        if k > 0:
-            for d in range(1, nz):
-                zone_part(k, d).wait_send()
+    others_of = [chip, chip_y, chip_x, chip_d]
+
+    def end_parts():
+        for k in range(PARTS):
+            for i in range(4):
+                at = dw_all.at[1 - core, others_of[i], rows_of(k)]
+                remote(at, at, send_k.at[k, i], recv_k.at[k, i], sibling).wait_recv()
+                share(k, others_of[i], send_k.at[k, i], recv_k.at[k, i], sibling, i == 0).wait_send()
+            share(k, chip, send_v.at[k], recv_v.at[k], partner, True).wait_send()
+            share(k, chip, send_h.at[k, 0], recv_h.at[k, 0], across, True).wait_send()
+            share(k, chip_y, send_h.at[k, 1], recv_h.at[k, 1], across).wait_send()
+            keep(k).wait()
+        line_end()
 
     groups = (pl.ds(0, lead), pl.ds(lead, width))
     order = [lax.rem(z + d, nz) for d in range(1, nz + 1)]
@@ -906,9 +858,47 @@
             acc = acc + got_z[n, :, cols].astype(F32)
         fin[:, cols] = acc.astype(BF)
 
+    line_slot(0, 0)
+    fetch = [pltpu.make_async_copy(gin_ref.at[j], dcat.at[pl.ds(j * capacity, capacity), 0:width], local.at[j]) for j in range(4)]
+    fetch.append(pltpu.make_async_copy(cot_ref, send_dx, local.at[4]))
+    fetch.append(pltpu.make_async_copy(att_ref, norm_t.at[:, 0:rows], local.at[5]))
+    fetch.append(pltpu.make_async_copy(res_ref.at[OWN], got_res.at[OWN], local.at[6]))
+    for c in fetch:
+        c.start()
+    results = {j: remote(res_ref.at[j], got_res.at[j], send_r.at[j], recv_r.at[j], plane[j]) for j in AWAY}
+    for c in fetch:
+        c.wait()
+    hidden = hidden_ref[...]
+    probs = probs_ref[...]
+    small = w_ref[:, own_cols:lead]
+    gain_two = small.astype(F32).T[EXPERTS + 1 : EXPERTS + 2, :]
+    lane = iota(probs.shape, 1)
+    back = None
+    grad_probs = jnp.zeros_like(probs)
+    for j in range(4):
+        pick = hot_cols(pick_col(places_ref[...], experts_of[j]), capacity)
+        add = nn(pick, dcat[j * capacity : (j + 1) * capacity, 0:width])
+        back = add if back is None else back + add
+        inner = jnp.sum(pick.astype(F32) * dot_ref[j][0:1, :], axis=1, keepdims=True)
+        grad_probs = jnp.where(lane == experts_of[j], inner, grad_probs)
+    mixed = jnp.sum(probs * grad_probs, axis=1, keepdims=True)
+    low = (probs * (grad_probs - mixed)).astype(BF)
+    r_two = lax.rsqrt(jnp.mean(hidden * hidden, axis=1, keepdims=True) + EPSILON)
+    h_norm = hidden * r_two
+    routed = (h_norm * gain_two).astype(BF)
+    grad_routed = back + nt(low, small)
+    dg_two = jnp.sum(grad_routed * h_norm, axis=0, keepdims=True)
+    u = grad_routed * gain_two
+    grad_hidden = send_dx[...].astype(F32) + r_two * (
+        u - h_norm * jnp.mean(u * h_norm, axis=1, keepdims=True)
+    )
+    gh[...] = grad_hidden
+    hid_low = grad_hidden.astype(BF)
+    gatt[...] = nt(hid_low, w_ref[:, lead:]).astype(BF)
+
     def give(p, to):
         return remote(
-            gatt_ref.at[:, pl.ds(al((1 - sq) * half + p * 128), 128)],
+            gatt.at[:, pl.ds(al((1 - sq) * half + p * 128), 128)],
             grad.at[p, pl.ds(to, rows)],
             send_g.at[p],
             recv_g.at[p],
@@ -917,10 +907,11 @@
 
     for p in range(pairs):
         give(p, base).start()
-    start_part(1)
+    line_slot(1, 0)
     for p in range(pairs):
-        grad[p, pl.ds(base, rows), :] = gatt_ref[:, pl.ds(al(sq * half + p * 128), 128)]
-    sums[:, cols_of(1)] = dout_ref[...]
+        grad[p, pl.ds(base, rows), :] = gatt[:, pl.ds(al(sq * half + p * 128), 128)]
+    d_route = tn(routed, low)
+    sums[:, cols_of(1)] = tn(norm_t[:, 0:rows], hid_low).astype(BF)
     for n in range(nz):
         for i in range(2):
             to_core(1, n, i).start()
@@ -936,6 +927,7 @@
         at = slice(i * rows, (i + 1) * rows)
         norm_t[:, at] = (norm_of(at)[0] * gain).astype(BF).T
 
+    line_slot(0, 1)
     blocks = 2 * rows // QB
     scale = HEAD_DIM ** (-0.5)
     zero = jnp.zeros((), BF)
@@ -979,18 +971,26 @@
 
         @pl.when(p == 0)
         def _():
-            sum_part(0)
-            start_part(2)
+            line_slot(2, 0)
+            for c in results.values():
+                c.start()
+            line_slot(0, 2)
             for n in range(nz):
                 reduce_core(1, n)
 
         @pl.when(p == 1)
         def _():
-            pass_part(0)
-            sum_part(1)
-            start_part(3)
+            line_slot(3, 0)
+            line_slot(1, 1)
+            sum_part(0)
             for n in range(nz - 1):
                 reduce_x(1, n)
+
+        @pl.when(p == 2)
+        def _():
+            line_slot(1, 2)
+            line_slot(2, 1)
+            pass_part(0)
 
     partial = nt(dcat[pl.ds(there, rows), :], w_ref[:, 0:own_cols])
     send_dx[...] = partial.astype(BF)
@@ -1000,9 +1000,9 @@
     partial = nt(dcat[pl.ds(base, rows), :], w_ref[:, 0:own_cols])
     own_gn[...] = partial
     dg_one = dg_one + jnp.sum(partial * norm_of(pl.ds(base, rows))[0], axis=0, keepdims=True)
-    stacked = jnp.concatenate([dg_one, dgain_ref[...], jnp.zeros((126, width), F32)], axis=0).T
+    stacked = jnp.concatenate([dg_one, dg_two, jnp.zeros((126, width), F32)], axis=0).T
     lane = iota((1, 128), 1)
-    small = jnp.where(lane < EXPERTS, droute_ref[...], 0.0)
+    small = jnp.where(lane < EXPERTS, d_route, 0.0)
     for i in range(2):
         small = jnp.where(lane == EXPERTS + i, stacked[:, i : i + 1], small)
     sums[:, own_cols:lead] = small.astype(BF)
@@ -1011,17 +1011,26 @@
         sums[zone, 0:own_cols] = nn(norm_t[zone, :], dcat[...]).astype(BF)
         for i in range(2):
             to_core(0, n, i).start()
-    pass_part(1)
-    sum_part(2)
-    last_part(0)
     reduce_core(0, 0)
     for n in range(1, nz):
         reduce_core(0, n)
+        if n == 1:
+            line_slot(2, 2)
+            sum_part(1)
         reduce_x(0, n - 1)
+    line_slot(3, 1)
+    last_part(0)
+    pass_part(1)
     reduce_z(1, reduce_x(1, nz - 1))
-    last_part(1)
-    pass_part(2)
-    sum_part(3)
+    total_out = hidden_ref[...]
+    for j in (OWN,) + AWAY:
+        if j != OWN:
+            results[j].wait_recv()
+        pick = hot_cols(pick_col(places_ref[...], experts_of[j]), capacity)
+        total_out = total_out + pick_col(probs_ref[...], experts_of[j]) * nn(pick, got_res[j])
+    out_ref[...] = total_out.astype(BF)
+    sum_part(2)
+    line_slot(3, 2)
     reduce_z(0, reduce_x(0, nz - 1))
     to_f = remote(fin, got_f, send_f, recv_f, partner)
     to_f.start()
@@ -1029,10 +1038,10 @@
     grad_n = own_gn[...] + got_dx[...].astype(F32)
     x_norm, r_one = norm_of(pl.ds(base, rows))
     u = grad_n * gain
-    dx = gh_ref[...] + r_one * (u - x_norm * jnp.mean(u * x_norm, axis=1, keepdims=True))
+    dx = gh[...] + r_one * (u - x_norm * jnp.mean(u * x_norm, axis=1, keepdims=True))
     dx_ref[...] = dx.astype(BF)
-    pass_part(3)
-    last_part(2)
+    last_part(1)
+    pass_part(2)
     to_f.wait_recv()
 
     def spot(px, co):
@@ -1050,6 +1059,9 @@
 
     pass_on(x, core, send_a, recv_a, across).start()
     pass_on(x, core, send_b.at[0], recv_b.at[0], sibling).start()
+    sum_part(3)
+    last_part(2)
+    pass_part(3)
     pass_on(1 - x, core, send_a, recv_a, across).wait_recv()
     pass_on(1 - x, core, send_b.at[1], recv_b.at[1], sibling).start()
     pass_on(x, 1 - core, send_b.at[0], recv_b.at[0], sibling).wait_recv()
@@ -1060,8 +1072,9 @@
     dgains_out[...] = small[:, EXPERTS : EXPERTS + 2]
     dout_out[...] = total[:, 3 * width + 128 :].astype(F32)
     last_part(3)
-    for k in range(PARTS):
-        end_part(k)
+    end_parts()
+    for c in results.values():
+        c.wait_send()
     pass_on(x, core, send_a, recv_a, across).wait_send()
     pass_on(x, core, send_b.at[0], recv_b.at[0], sibling).wait_send()
     pass_on(1 - x, core, send_b.at[1], recv_b.at[1], sibling).wait_send()
@@ -1078,30 +1091,40 @@
         give(p, base).wait_send()
 
 
-def finish(xs, grad_att, qkv, mixed, lse, whole, grad_hidden, d_out, d_route, d_gain, segments, dw_half, dw_first, prompt, nz, cid):
-    rows, width = grad_att.shape
+def finish(
+    xs, qkv, mixed, lse, whole, segments, hidden, probs, places, inner, gin, res, cot, attended, dw_half,
+    prompt, nz, capacity, cid,
+):
+    rows, width = cot.shape
     pairs = width // 256
     cols = whole.shape[1]
     shard = width // nz
     part = shard // 4
     group = 2 * rows
+    deep = dw_half.shape[1]
+    quarter = (deep // PARTS, dw_half.shape[2])
     dma = pltpu.SemaphoreType.DMA
     two = lambda *shape: [dma(shape), dma(shape)]
     vm = pltpu.VMEM
     return pl.pallas_call(
-        functools.partial(finish_kernel, prompt, nz),
+        functools.partial(finish_kernel, prompt, nz, capacity),
         out_shape=(
+            sds((rows, width), BF),
             sds((rows, width), BF),
             sds((shard, 3 * width), F32),
             sds((shard, width), F32),
             sds((shard, EXPERTS), F32),
             sds((shard, 2), F32),
-            sds((PARTS - 1,) + dw_first.shape, BF),
+            sds((PARTS, nz) + quarter, BF),
+            sds((PARTS, nz) + quarter, BF),
             sds((2, 4) + dw_half.shape[1:], BF),
         ),
-        in_specs=[VM] * 11 + [ANY, ANY],
-        out_specs=(VM,) * 5 + (ANY, ANY),
+        in_specs=[VM] * 10 + [ANY] * 5,
+        out_specs=(VM,) * 6 + (ANY,) * 3,
         scratch_shapes=[
+            vm((rows, width), F32),
+            vm((rows, width), BF),
+            vm((4, capacity, width), BF),
             vm((pairs, group, 128), BF),
             vm((2, group, 128), BF),
             vm((2, group, 128), BF),
@@ -1120,20 +1143,24 @@
             vm((rows, width), BF),
             vm((rows, width), BF),
             vm((rows, width), F32),
-            vm((nz,) + dw_first.shape[1:], BF),
-            vm((PARTS,) + dw_first.shape[1:], BF),
+            vm((nz,) + quarter, BF),
+            vm((PARTS,) + quarter, BF),
+            vm((2, 3) + quarter, BF),
             dma((nz + PARTS,)),
         ]
-        + two(pairs) + two(2, nz, 2) + two(2, nz) + two(2, nz - 1) + two() + two() + two() + two(2)
-        + two(PARTS - 1, nz - 1) + two(PARTS) + two(PARTS, 2) + two(PARTS, 4),
+        + two(4) + two(pairs) + two(2, nz, 2) + two(2, nz) + two(2, nz - 1) + two() + two() + two() + two(2)
+        + two(PARTS, nz) + two(PARTS, nz) + two(PARTS) + two(PARTS, 2) + two(PARTS, 4),
         compiler_params=params(cid),
         name="finish",
-    )(xs, grad_att, qkv, mixed, lse, whole, grad_hidden, d_out, d_route, d_gain, segments, dw_half, dw_first)
+    )(xs, qkv, mixed, lse, whole, segments, hidden, probs, places, inner, gin, res, cot, attended, dw_half)
 
 
 def spread_kernel(in_ref, out_ref):
-    for e in range(EXPERTS):
-        out_ref[:, e, :] = in_ref[e].astype(F32)
+    rows, experts_, k = out_ref.shape
+    flat = rows * experts_
+    at, of = iota((flat, flat), 0), iota((flat, flat), 1)
+    move = (of == lax.rem(at, experts_) * rows + at // experts_).astype(F32).astype(BF)
+    out_ref[...] = nn(move, in_ref[...].reshape(flat, k)).reshape(rows, experts_, k)
 
 
 def spread_experts(parts):
@@ -1170,12 +1197,9 @@
     hidden, probs, gin, res, inner, dw_half = experts(
         x, attended, whole, places_row, places_col, raw, near, capacity, nz, 1
     )
-    block_out, grad_hidden, grad_att, d_out, d_route, d_gain_two, dw_first = after(
-        gin, res, inner, hidden, probs, places_col, cot, whole, attended, dw_half, capacity, 2
-    )
-    d_tokens, d_in, d_out, d_route, d_gains, _, dw_all = finish(
-        xs, grad_att, qkv, mixed, lse, whole, grad_hidden, d_out, d_route, d_gain_two, segments, dw_half, dw_first,
-        prompt, nz, 3,
+    block_out, d_tokens, d_in, d_out, d_route, d_gains, _, _, dw_all = finish(
+        xs, qkv, mixed, lse, whole, segments, hidden, probs, places_col, inner, gin, res, cot, attended, dw_half,
+        prompt, nz, capacity, 2,
     )
     d_expert = spread_experts(dw_all)
     return (

time: 405 us -> 373 us (0.921)
  Pallas kernels: 381 us -> 349 us
    pallas_call x2 -> x1, Pallas kernels: 190 us -> 155 us  [finish(): pl.pallas_call(functools.partial(finish_kernel, prompt, nz, capacity), ou...]
where the time goes in v1:
time: 373 us; the launch traced here: 367 us
  Pallas kernels  349 us (94%)
  local copies, waits for them, and re-layouts  17.8 us (5%)
    pallas_call x1, Pallas kernels, finish(): pl.pallas_call(functools.partial(finish_kernel, prompt, nz, capacity), ou...  155 us
    pallas_call x1, Pallas kernels, experts(): pl.pallas_call(functools.partial(experts_kernel, capacity, nz), out_shape...  101 us
    pallas_call x1, Pallas kernels, begin(): pl.pallas_call(functools.partial(begin_kernel, prompt, nz, capacity), out...  76.3 us
    pallas_call x1, Pallas kernels, spread_experts(): pl.pallas_call(spread_kernel, grid=(cores, 8), out_shape=sds((cores * r,...  16.3 us
    unnamed x18, local copies, waits for them, and re-layouts  13.1 us

profile of v1, /device:TPU:9, one launch (start us, length us, event | category | flops | bytes accessed | tf_op | source)
XLA Modules:
  0.0 367.3 jit_solution(13862310791511759792)
XLA Ops:
  0.7 1.4 copy.23.router_ref
  2.1 1.4 copy.24.gains_ref
  3.5 1.6 copy.21
  5.1 4.8 %constant_dynamic-slice_fusion = bf16[384,1,1536]{2,1,0:T(2,128)(2,1)S(1)} fusion(bf16[768,4,1536]{2,1,0:T(4,128)(2,1)} %param.14, s32[]{:T(128)S(6)} %select_n.11, s32[]{:T(128)S(6)} %select_n.13), kind=kLoop, calls=%fused_computation.1 | loop fusion | bytes 2359304 | tf_op jit(solution)/shard_map/dynamic_slice | solution.py:1193
  9.9 1.2 copy.29
  11.1 76.3 %begin.1 = (bf16[1536,768]{1,0:T(8,128)(2,1)}, bf16[768,2048]{1,0:T(8,128)(2,1)}, bf16[3,3,1536,128]{3,2,1,0:T(8,128)(2,1)}, bf16[3,1536,128]{2,1,0:T(8,128)(2,1...) custom-call(bf16[768,768]{1,0:T(8,128)(2,1)} %bitcast.11, ...), custom_call_target="tpu_custom_call" | custom-call | tf_op jit(solution)/shard_map/begin/pallas_call | solution.py:348
  87.4 100.5 %experts.1 = (f32[768,768]{1,0:T(8,128)}, f32[768,128]{1,0:T(8,128)}, bf16[4,384,768]{2,1,0:T(8,128)(2,1)}, bf16[4,384,768]{2,1,0:T(8,128)(2,1)}, f32[4,8,384]{2,1,0:T(8,128)}, /*index=5*/bf16[4,384,1536]{2,1,0:T(8,128)(2,1)}) custom-call(bf16[768,768]{1,0:T(8,128)(2,1)} %bitcast.12, bf16[768,768]{1,0:T(8,128)(2,1)} %get-tuple-element.35.att_ref, ...), custom_call_target="tpu_custom_call" | custom-call | tf_op jit(solution)/shard_map/experts/pallas_call | solution.py:634
  187.9 155.4 %finish.1 = (bf16[768,768]{1,0:T(8,128)(2,1)}, bf16[768,768]{1,0:T(8,128)(2,1)}, f32[192,2304]{1,0:T(8,128)}, f32[192,768]{1,0:T(8,128)}, f32[192,4]{1,0:T(8,128...) custom-call(bf16[1536,768]{1,0:T(8,128)(2,1)} %get-tuple-element.30., ...), custom_call_target="tpu_custom_call" | custom-call | tf_op jit(solution)/shard_map/finish/pallas_call | solution.py:1109
  343.4 1.6 copy.26
  344.9 1.6 copy.25
  346.5 0.0 copy-start.2
  346.5 0.0 copy-start.1
  346.5 16.3 %spread.1 = f32[768,4,1536]{2,1,0:T(4,128)} custom-call(bf16[2,4,384,1536]{3,2,1,0:T(8,128)(2,1)} %get-tuple-element.52.in_ref), custom_call_target="tpu_custom_call" | custom-call | tf_op jit(solution)/shard_map/spread/pallas_call | solution.py:1169
  362.8 0.0 copy-done.2
  362.8 0.0 copy-start
  362.8 1.0 copy.34
  363.8 0.0 copy-done.1
  363.8 1.0 copy.35
  364.8 0.0 copy-done
  364.8 0.0 copy-start.3
  364.8 1.2 copy.36
  366.0 0.3 copy-done.3
  366.3 0.8 copy.37
Async XLA Ops:
  346.5 16.3 %copy-start.2 = (bf16[768,768]{1,0:T(8,128)(2,1)S(1)}, bf16[768,768]{1,0:T(8,128)(2,1)}, u32[]{:S(2)}) copy-start(bf16[768,768]{1,0:T(8,128)(2,1)} %get-tuple-element.46) | copy-start | bytes 3538948
  346.5 17.3 %copy-start.1 = (bf16[768,768]{1,0:T(8,128)(2,1)S(1)}, bf16[768,768]{1,0:T(8,128)(2,1)}, u32[]{:S(2)}) copy-start(bf16[768,768]{1,0:T(8,128)(2,1)} %get-tuple-element.47) | copy-start | bytes 3538948
  362.8 2.0 copy-start
  364.8 1.5 copy-start.3

commit v2 on v1

--- a/solution.py
+++ b/solution.py
@@ -180,11 +180,14 @@
 
     packs = [
         pltpu.make_async_copy(
-            in_ref.at[:, pl.ds(al(i * width + sq * half), half)], pack.at[:, pl.ds(i * half, half)], local.at[i]
+            in_ref.at[:, pl.ds(al(i * width + sq * half + p * 128), 128)],
+            pack.at[:, pl.ds((3 * p + i) * 128, 128)],
+            local.at[3 * p + i],
         )
+        for p in range(pairs)
         for i in range(3)
     ]
-    packs.append(pltpu.make_async_copy(out_ref, pack.at[:, groups[1]], local.at[3]))
+    packs.append(pltpu.make_async_copy(out_ref, pack.at[:, groups[1]], local.at[3 * pairs]))
     for c in packs:
         c.start()
     lane = iota((1, 128), 1)
@@ -220,7 +223,7 @@
 
     for d in range(1, nz):
         along(d, 0).start()
-    own = pltpu.make_async_copy(pack, w_ref.at[pl.ds(pl.multiple_of(z * shard, shard), shard)], local.at[4])
+    own = pltpu.make_async_copy(pack, w_ref.at[pl.ds(pl.multiple_of(z * shard, shard), shard)], local.at[3 * pairs + 1])
     own.start()
     xs_ref[pl.ds(base, rows), :] = x_ref[...]
     ids = ids_ref[...]
@@ -249,7 +252,7 @@
             for i in range(2):
                 beside(d, g, i, 1 - core).wait_recv()
 
-    stay = pltpu.make_async_copy(piece_ref, near_ref.at[z], local.at[5])
+    stay = pltpu.make_async_copy(piece_ref, near_ref.at[z], local.at[3 * pairs + 2])
     stay.start()
     line = Line(
         nz, dp, sq, z, lambda stage, zone: piece_ref if stage == 1 else near_ref.at[zone], near_ref, line_sems
@@ -262,10 +265,10 @@
     gain = w_ref[:, own_cols:lead].astype(F32).T[EXPERTS : EXPERTS + 1, :]
     xf = xs_ref[...].astype(F32)
     normed = (xf * lax.rsqrt(jnp.mean(xf * xf, axis=1, keepdims=True) + EPSILON) * gain).astype(BF)
-    for i in range(3):
-        got = nn(normed, w_ref[:, i * half : (i + 1) * half]).astype(BF)
-        for p in range(pairs):
-            qkv_ref[p, i] = got[:, p * 128 : (p + 1) * 128]
+    for p in range(pairs):
+        got = nn(normed, w_ref[:, p * 384 : (p + 1) * 384]).astype(BF)
+        for i in range(3):
+            qkv_ref[p, i] = got[:, i * 128 : (i + 1) * 128]
 
     blocks = 2 * rows // QB
     const = HEAD_DIM ** (-0.5) * LOG2E
@@ -364,7 +367,7 @@
         scratch_shapes=[
             pltpu.VMEM((shard, cols), BF),
             pltpu.VMEM((144, 2 * rows), BF),
-            dma((6,)),
+            dma((3 * pairs + 3,)),
         ]
         + two() + two(nz - 1, 2) + two(nz - 1, 2) + two(nz - 1, 2, 2) + two(pairs) + two(2) + two(2),
         compiler_params=params(cid),
@@ -811,7 +814,8 @@
             keep(k).wait()
         line_end()
 
-    groups = (pl.ds(0, lead), pl.ds(lead, width))
+    spans = [((pairs - 1) * 384, lead), (lead, lead + width)] + [(p * 384, (p + 1) * 384) for p in range(pairs - 1)]
+    groups = [pl.ds(lo, hi - lo) for lo, hi in spans]
     order = [lax.rem(z + d, nz) for d in range(1, nz + 1)]
 
     def piece(zz, px, co):
@@ -831,7 +835,7 @@
         )
 
     def cols_of(g):
-        return slice(0, lead) if g == 0 else slice(lead, lead + width)
+        return slice(*spans[g])
 
     def reduce_core(g, n):
         cols = cols_of(g)
@@ -866,6 +870,8 @@
     for c in fetch:
         c.start()
     results = {j: remote(res_ref.at[j], got_res.at[j], send_r.at[j], recv_r.at[j], plane[j]) for j in AWAY}
+    for j in range(OWN):
+        results[j].start()
     for c in fetch:
         c.wait()
     hidden = hidden_ref[...]
@@ -928,6 +934,14 @@
         norm_t[:, at] = (norm_of(at)[0] * gain).astype(BF).T
 
     line_slot(0, 1)
+    def weight_grad(g, p):
+        cols = slice(p * 384, (p + 1) * 384)
+        for n in range(nz):
+            zone = pl.ds(pl.multiple_of(order[n] * shard, shard), shard)
+            sums[zone, cols] = nn(norm_t[zone, :], dcat[:, cols]).astype(BF)
+            for i in range(2):
+                to_core(g, n, i).start()
+
     blocks = 2 * rows // QB
     scale = HEAD_DIM ** (-0.5)
     zero = jnp.zeros((), BF)
@@ -965,32 +979,39 @@
                     dk = b if dk is None else dk + b
                     to = slice(h * HEAD_DIM, (h + 1) * HEAD_DIM)
                     dqt[to, at] = c if j == 0 else dqt[to, at] + c
-            dcat[keys, pl.ds(al(half + p * 128), 128)] = dk.astype(BF)
-            dcat[keys, pl.ds(al(2 * half + p * 128), 128)] = dv.astype(BF)
-        dcat[:, pl.ds(al(p * 128), 128)] = (dqt[...] * scale).T.astype(BF)
+            dcat[keys, pl.ds(al(p * 384 + 128), 128)] = dk.astype(BF)
+            dcat[keys, pl.ds(al(p * 384 + 256), 128)] = dv.astype(BF)
+        dcat[:, pl.ds(al(p * 384), 128)] = (dqt[...] * scale).T.astype(BF)
 
         @pl.when(p == 0)
         def _():
+            weight_grad(2, 0)
             line_slot(2, 0)
-            for c in results.values():
-                c.start()
+            results[3].start()
             line_slot(0, 2)
             for n in range(nz):
                 reduce_core(1, n)
 
         @pl.when(p == 1)
         def _():
+            weight_grad(3, 1)
             line_slot(3, 0)
             line_slot(1, 1)
             sum_part(0)
             for n in range(nz - 1):
                 reduce_x(1, n)
+            for n in range(nz):
+                reduce_core(2, n)
 
         @pl.when(p == 2)
         def _():
             line_slot(1, 2)
             line_slot(2, 1)
             pass_part(0)
+            for n in range(nz):
+                reduce_core(3, n)
+            for n in range(nz - 1):
+                reduce_x(2, n)
 
     partial = nt(dcat[pl.ds(there, rows), :], w_ref[:, 0:own_cols])
     send_dx[...] = partial.astype(BF)
@@ -1006,11 +1027,7 @@
     for i in range(2):
         small = jnp.where(lane == EXPERTS + i, stacked[:, i : i + 1], small)
     sums[:, own_cols:lead] = small.astype(BF)
-    for n in range(nz):
-        zone = pl.ds(pl.multiple_of(order[n] * shard, shard), shard)
-        sums[zone, 0:own_cols] = nn(norm_t[zone, :], dcat[...]).astype(BF)
-        for i in range(2):
-            to_core(0, n, i).start()
+    weight_grad(0, pairs - 1)
     reduce_core(0, 0)
     for n in range(1, nz):
         reduce_core(0, n)
@@ -1018,10 +1035,13 @@
             line_slot(2, 2)
             sum_part(1)
         reduce_x(0, n - 1)
+    for n in range(nz - 1):
+        reduce_x(3, n)
     line_slot(3, 1)
     last_part(0)
     pass_part(1)
-    reduce_z(1, reduce_x(1, nz - 1))
+    for g in (1, 2):
+        reduce_z(g, reduce_x(g, nz - 1))
     total_out = hidden_ref[...]
     for j in (OWN,) + AWAY:
         if j != OWN:
@@ -1031,6 +1051,7 @@
     out_ref[...] = total_out.astype(BF)
     sum_part(2)
     line_slot(3, 2)
+    reduce_z(3, reduce_x(3, nz - 1))
     reduce_z(0, reduce_x(0, nz - 1))
     to_f = remote(fin, got_f, send_f, recv_f, partner)
     to_f.start()
@@ -1048,10 +1069,11 @@
         return pl.ds(pl.multiple_of((px * 2 + co) * part, part), part)
 
     here = spot(x, core)
-    for i in range(3):
-        cols = slice(i * half, (i + 1) * half)
-        total[here, pl.ds(al(i * width + sq * half), half)] = fin[:, cols]
-        total[here, pl.ds(al(i * width + (1 - sq) * half), half)] = got_f[:, cols]
+    for p in range(pairs):
+        for i in range(3):
+            cols = slice((3 * p + i) * 128, (3 * p + i + 1) * 128)
+            total[here, pl.ds(al(i * width + sq * half + p * 128), 128)] = fin[:, cols]
+            total[here, pl.ds(al(i * width + (1 - sq) * half + p * 128), 128)] = got_f[:, cols]
     total[here, 3 * width :] = (fin[:, own_cols:].astype(F32) + got_f[:, own_cols:].astype(F32)).astype(BF)
 
     def pass_on(px, co, send, recv, peer):
@@ -1080,7 +1102,7 @@
     pass_on(1 - x, core, send_b.at[1], recv_b.at[1], sibling).wait_send()
     to_f.wait_send()
     to_dx.wait_send()
-    for g in range(2):
+    for g in range(len(spans)):
         for n in range(nz):
             for i in range(2):
                 to_core(g, n, i).wait_send()
@@ -1148,7 +1170,7 @@
             vm((2, 3) + quarter, BF),
             dma((nz + PARTS,)),
         ]
-        + two(4) + two(pairs) + two(2, nz, 2) + two(2, nz) + two(2, nz - 1) + two() + two() + two() + two(2)
+        + two(4) + two(pairs) + two(pairs + 1, nz, 2) + two(pairs + 1, nz) + two(pairs + 1, nz - 1) + two() + two() + two() + two(2)
         + two(PARTS, nz) + two(PARTS, nz) + two(PARTS) + two(PARTS, 2) + two(PARTS, 4),
         compiler_params=params(cid),
         name="finish",
@@ -1156,22 +1178,19 @@
 
 
 def spread_kernel(in_ref, out_ref):
-    rows, experts_, k = out_ref.shape
-    flat = rows * experts_
-    at, of = iota((flat, flat), 0), iota((flat, flat), 1)
-    move = (of == lax.rem(at, experts_) * rows + at // experts_).astype(F32).astype(BF)
-    out_ref[...] = nn(move, in_ref[...].reshape(flat, k)).reshape(rows, experts_, k)
+    for e in range(EXPERTS):
+        out_ref[:, e, :] = in_ref[e].astype(F32)
 
 
 def spread_experts(parts):
     cores, experts_, r, k = parts.shape
-    block = r // 8
+    block = r // 2
     return pl.pallas_call(
         spread_kernel,
-        grid=(cores, 8),
+        grid=(cores, r // block),
         out_shape=sds((cores * r, experts_, k), F32),
         in_specs=[pl.BlockSpec((None, experts_, block, k), lambda c, i: (c, 0, i, 0))],
-        out_specs=pl.BlockSpec((block, experts_, k), lambda c, i: (c * 8 + i, 0, 0)),
+        out_specs=pl.BlockSpec((block, experts_, k), lambda c, i: (c * (r // block) + i, 0, 0)),
         compiler_params=params(),
         name="spread",
     )(parts)

time: 373 us -> 364 us (0.976)
  Pallas kernels: 349 us -> 341 us
    pallas_call x1, Pallas kernels: 16.3 us -> 12 us  [spread_experts(): pl.pallas_call(spread_kernel, grid=(cores, r // block), out_shape=sds((co...]
where the time goes in v2:
time: 364 us; the launch traced here: 360 us
  Pallas kernels  341 us (94%)
  local copies, waits for them, and re-layouts  17.8 us (5%)
    pallas_call x1, Pallas kernels, finish(): pl.pallas_call(functools.partial(finish_kernel, prompt, nz, capacity), ou...  152 us
    pallas_call x1, Pallas kernels, experts(): pl.pallas_call(functools.partial(experts_kernel, capacity, nz), out_shape...  101 us
    pallas_call x1, Pallas kernels, begin(): pl.pallas_call(functools.partial(begin_kernel, prompt, nz, capacity), out...  76.3 us
    unnamed x18, local copies, waits for them, and re-layouts  13.1 us
    pallas_call x1, Pallas kernels, spread_experts(): pl.pallas_call(spread_kernel, grid=(cores, r // block), out_shape=sds((co...  12 us

profile of v2, /device:TPU:9, one launch (start us, length us, event | category | flops | bytes accessed | tf_op | source)
XLA Modules:
  0.0 359.7 jit_solution(8990463352296834836)
XLA Ops:
  0.7 1.4 copy.23.router_ref
  2.1 1.4 copy.24.gains_ref
  3.5 1.6 copy.21
  5.1 4.8 %constant_dynamic-slice_fusion = bf16[384,1,1536]{2,1,0:T(2,128)(2,1)S(1)} fusion(bf16[768,4,1536]{2,1,0:T(4,128)(2,1)} %param.14, s32[]{:T(128)S(6)} %select_n.11, s32[]{:T(128)S(6)} %select_n.13), kind=kLoop, calls=%fused_computation.1 | loop fusion | bytes 2359304 | tf_op jit(solution)/shard_map/dynamic_slice | solution.py:1212
  9.9 1.2 copy.29
  11.1 76.3 %begin.1 = (bf16[1536,768]{1,0:T(8,128)(2,1)}, bf16[768,2048]{1,0:T(8,128)(2,1)}, bf16[3,3,1536,128]{3,2,1,0:T(8,128)(2,1)}, bf16[3,1536,128]{2,1,0:T(8,128)(2,1...) custom-call(bf16[768,768]{1,0:T(8,128)(2,1)} %bitcast.11, ...), custom_call_target="tpu_custom_call" | custom-call | tf_op jit(solution)/shard_map/begin/pallas_call | solution.py:351
  87.4 100.8 %experts.1 = (f32[768,768]{1,0:T(8,128)}, f32[768,128]{1,0:T(8,128)}, bf16[4,384,768]{2,1,0:T(8,128)(2,1)}, bf16[4,384,768]{2,1,0:T(8,128)(2,1)}, f32[4,8,384]{2,1,0:T(8,128)}, /*index=5*/bf16[4,384,1536]{2,1,0:T(8,128)(2,1)}) custom-call(bf16[768,768]{1,0:T(8,128)(2,1)} %bitcast.12, bf16[768,768]{1,0:T(8,128)(2,1)} %get-tuple-element.35.att_ref, ...), custom_call_target="tpu_custom_call" | custom-call | tf_op jit(solution)/shard_map/experts/pallas_call | solution.py:637
  188.2 151.9 %finish.1 = (bf16[768,768]{1,0:T(8,128)(2,1)}, bf16[768,768]{1,0:T(8,128)(2,1)}, f32[192,2304]{1,0:T(8,128)}, f32[192,768]{1,0:T(8,128)}, f32[192,4]{1,0:T(8,128...) custom-call(bf16[1536,768]{1,0:T(8,128)(2,1)} %get-tuple-element.30., ...), custom_call_target="tpu_custom_call" | custom-call | tf_op jit(solution)/shard_map/finish/pallas_call | solution.py:1131
  340.1 1.6 copy.26
  341.7 1.6 copy.25
  343.2 0.0 copy-start.2
  343.2 0.0 copy-start.1
  343.2 12.0 %spread.1 = f32[768,4,1536]{2,1,0:T(4,128)} custom-call(bf16[2,4,384,1536]{3,2,1,0:T(8,128)(2,1)} %get-tuple-element.52.in_ref), custom_call_target="tpu_custom_call" | custom-call | tf_op jit(solution)/shard_map/spread/pallas_call | solution.py:1188
  355.2 0.0 copy-done.2
  355.2 0.0 copy-start
  355.2 1.0 copy.34
  356.2 0.0 copy-done.1
  356.2 1.0 copy.35
  357.2 0.0 copy-done
  357.2 0.0 copy-start.3
  357.2 1.2 copy.36
  358.4 0.3 copy-done.3
  358.7 0.8 copy.37
Async XLA Ops:
  343.2 12.0 %copy-start.2 = (bf16[768,768]{1,0:T(8,128)(2,1)S(1)}, bf16[768,768]{1,0:T(8,128)(2,1)}, u32[]{:S(2)}) copy-start(bf16[768,768]{1,0:T(8,128)(2,1)} %get-tuple-element.46) | copy-start | bytes 3538948
  343.2 13.0 %copy-start.1 = (bf16[768,768]{1,0:T(8,128)(2,1)S(1)}, bf16[768,768]{1,0:T(8,128)(2,1)}, u32[]{:S(2)}) copy-start(bf16[768,768]{1,0:T(8,128)(2,1)} %get-tuple-element.47) | copy-start | bytes 3538948
  355.2 2.0 copy-start
  357.2 1.5 copy-start.3

commit v3 on v2

--- a/solution.py
+++ b/solution.py
@@ -674,11 +674,11 @@
 
 
 def finish_kernel(
-    prompt, nz, capacity, xs_ref, qkv_ref, mixed_ref, lse_ref, w_ref, seg_ref, hidden_ref, probs_ref, places_ref,
-    dot_ref, gin_ref, res_ref, cot_ref, att_ref, part_ref,
-    out_ref, dx_ref, din_out, dout_out, droute_out, dgains_out, got_up, got_down, dw_all,
-    gh, gatt, got_res, grad, qm, dom, kt, dqt, dcat, norm_t, sums, got_c, got_x, got_z, mine, fin, got_f, total,
-    send_dx, got_dx, own_gn, stage, dw_sum, ahead,
+    prompt, nz, capacity, xs_ref, lse_ref, w_ref, seg_ref, hidden_ref, probs_ref, places_ref,
+    dot_ref, qkv_hbm, mixed_hbm, gin_ref, res_ref, cot_ref, att_ref, part_ref,
+    out_ref, dx_ref, din_out, dout_out, droute_out, dgains_out, dw_all,
+    gh, gatt, got_res, qkv_ref, mixed_ref, grad, qm, dom, kt, dqt, dcat, norm_t, sums, got_c, got_x, got_z, mine, fin, got_f, total,
+    send_dx, got_dx, own_gn, stage, dw_sum, ahead, got_up, got_down,
     local, send_r, recv_r, send_g, recv_g, send_c, recv_c, send_x, recv_x, send_z, recv_z, send_d, recv_d, send_f, recv_f,
     send_a, recv_a, send_b, recv_b, send_u, recv_u, send_l, recv_l, send_v, recv_v, send_h, recv_h, send_k, recv_k,
 ):
@@ -711,7 +711,7 @@
     def hop(k, t, up, src):
         to = lax.rem(z + 1, nz) if up else lax.rem(z + nz - 1, nz)
         got, send, recv = (got_up, send_u, recv_u) if up else (got_down, send_l, recv_l)
-        return remote(src, got.at[k, t], send.at[k, t], recv.at[k, t], (dp, sq, to))
+        return remote(src, got.at[k, t - 1 if up else t], send.at[k, t], recv.at[k, t], (dp, sq, to))
 
     def legs(slot):
         ups = (True, slot, list(range(nz - 1, slot, -1)))
@@ -727,21 +727,20 @@
                     for t in zones:
                         hop(k, t, up, part_ref.at[t, rows_of(k)]).start()
                     return
-                got = got_up if up else got_down
-                loads = []
-                for i, t in enumerate(zones):
-                    hop(k, t, up, ahead.at[k % 2, 0]).wait_recv()
-                    loads.append(pltpu.make_async_copy(got.at[k, t], stage.at[2 * i], local.at[2 * i]))
-                    loads.append(pltpu.make_async_copy(part_ref.at[t, rows_of(k)], stage.at[2 * i + 1], local.at[2 * i + 1]))
+                loads = [
+                    pltpu.make_async_copy(part_ref.at[t, rows_of(k)], stage.at[i], local.at[i])
+                    for i, t in enumerate(zones)
+                ]
                 for c in loads:
                     c.start()
                 for i, t in enumerate(zones):
                     to = ahead.at[k % 2, i if slot == 1 else 2]
                     if k > 1:
                         hop(k - 2, t, up, to).wait_send()
-                    loads[2 * i].wait()
-                    loads[2 * i + 1].wait()
-                    to[...] = (stage[2 * i].astype(F32) + stage[2 * i + 1].astype(F32)).astype(BF)
+                    hop(k, t, up, to).wait_recv()
+                    loads[i].wait()
+                    got = got_up[k, t - 1] if up else got_down[k, t]
+                    to[...] = (stage[i].astype(F32) + got.astype(F32)).astype(BF)
                     hop(k, t, up, to).start()
 
     def line_end():
@@ -767,23 +766,23 @@
     def sum_part(k):
         own = pltpu.make_async_copy(part_ref.at[z, rows_of(k)], stage.at[2], local.at[2])
         own.start()
-        for i, up in enumerate((True, False)):
-            got = got_up if up else got_down
-            has = z > 0 if up else z < nz - 1
-
-            @pl.when(has)
-            def _(i=i, up=up, got=got):
-                hop(k, z, up, ahead.at[0, 0]).wait_recv()
-                c = pltpu.make_async_copy(got.at[k, z], stage.at[i], local.at[i])
-                c.start()
-                c.wait()
-
-            @pl.when(jnp.logical_not(has))
-            def _(i=i):
-                stage[i] = jnp.zeros(stage.shape[1:], BF)
+        above_zero, below_top = z > 0, z < nz - 1
+
+        @pl.when(above_zero)
+        def _():
+            hop(k, z, True, ahead.at[0, 0]).wait_recv()
+            stage[0] = got_up[k, z - 1]
+
+        @pl.when(below_top)
+        def _():
+            hop(k, z, False, ahead.at[0, 0]).wait_recv()
+            stage[1] = got_down[k, z]
 
         own.wait()
-        dw_sum[k] = (stage[0].astype(F32) + stage[1].astype(F32) + stage[2].astype(F32)).astype(BF)
+        acc = stage[2].astype(F32)
+        acc = acc + jnp.where(above_zero, stage[0].astype(F32), 0.0)
+        acc = acc + jnp.where(below_top, stage[1].astype(F32), 0.0)
+        dw_sum[k] = acc.astype(BF)
         share(k, chip, send_v.at[k], recv_v.at[k], partner, True).start()
         share(k, chip, send_h.at[k, 0], recv_h.at[k, 0], across, True).start()
         share(k, chip, send_k.at[k, 0], recv_k.at[k, 0], sibling, True).start()
@@ -862,6 +861,14 @@
             acc = acc + got_z[n, :, cols].astype(F32)
         fin[:, cols] = acc.astype(BF)
 
+    def pair_loads(p):
+        return (
+            pltpu.make_async_copy(qkv_hbm.at[p], qkv_ref, local.at[nz + PARTS]),
+            pltpu.make_async_copy(mixed_hbm.at[p], mixed_ref, local.at[nz + PARTS + 1]),
+        )
+
+    for c in pair_loads(0):
+        c.start()
     line_slot(0, 0)
     fetch = [pltpu.make_async_copy(gin_ref.at[j], dcat.at[pl.ds(j * capacity, capacity), 0:width], local.at[j]) for j in range(4)]
     fetch.append(pltpu.make_async_copy(cot_ref, send_dx, local.at[4]))
@@ -949,18 +956,20 @@
     @pl.loop(0, pairs)
     def _(p):
         give(p, there).wait_recv()
-        kt[...] = qkv_ref[p, 1].T
-        prod = (grad[p].astype(F32) * mixed_ref[p].astype(F32)).T
+        for c in pair_loads(p):
+            c.wait()
+        kt[...] = qkv_ref[1].T
+        prod = (grad[p].astype(F32) * mixed_ref[...].astype(F32)).T
         delta = []
         for h in range(2):
             lanes = iota((1, 128), 1) // HEAD_DIM == h
-            qm[h] = jnp.where(lanes, qkv_ref[p, 0], zero) * jnp.asarray(scale, BF)
+            qm[h] = jnp.where(lanes, qkv_ref[0], zero) * jnp.asarray(scale, BF)
             dom[h] = jnp.where(lanes, grad[p], zero)
             low = h * HEAD_DIM
             delta.append(jnp.sum(prod[low : low + HEAD_DIM, :], axis=0, keepdims=True))
         for j in range(blocks):
             keys = slice(j * QB, (j + 1) * QB)
-            k, v = qkv_ref[p, 1, keys, :], qkv_ref[p, 2, keys, :]
+            k, v = qkv_ref[1, keys, :], qkv_ref[2, keys, :]
             dk = dv = None
             for i in range(j, blocks):
                 at = slice(i * QB, (i + 1) * QB)
@@ -982,6 +991,11 @@
             dcat[keys, pl.ds(al(p * 384 + 128), 128)] = dk.astype(BF)
             dcat[keys, pl.ds(al(p * 384 + 256), 128)] = dv.astype(BF)
         dcat[:, pl.ds(al(p * 384), 128)] = (dqt[...] * scale).T.astype(BF)
+
+        @pl.when(p < pairs - 1)
+        def _():
+            for c in pair_loads(p + 1):
+                c.start()
 
         @pl.when(p == 0)
         def _():
@@ -1137,16 +1151,16 @@
             sds((shard, width), F32),
             sds((shard, EXPERTS), F32),
             sds((shard, 2), F32),
-            sds((PARTS, nz) + quarter, BF),
-            sds((PARTS, nz) + quarter, BF),
             sds((2, 4) + dw_half.shape[1:], BF),
         ),
-        in_specs=[VM] * 10 + [ANY] * 5,
-        out_specs=(VM,) * 6 + (ANY,) * 3,
+        in_specs=[VM] * 8 + [ANY] * 7,
+        out_specs=(VM,) * 6 + (ANY,),
         scratch_shapes=[
             vm((rows, width), F32),
             vm((rows, width), BF),
             vm((4, capacity, width), BF),
+            vm((3, group, 128), BF),
+            vm((group, 128), BF),
             vm((pairs, group, 128), BF),
             vm((2, group, 128), BF),
             vm((2, group, 128), BF),
@@ -1168,13 +1182,15 @@
             vm((nz,) + quarter, BF),
             vm((PARTS,) + quarter, BF),
             vm((2, 3) + quarter, BF),
-            dma((nz + PARTS,)),
+            vm((PARTS, nz - 1) + quarter, BF),
+            vm((PARTS, nz - 1) + quarter, BF),
+            dma((nz + PARTS + 2,)),
         ]
         + two(4) + two(pairs) + two(pairs + 1, nz, 2) + two(pairs + 1, nz) + two(pairs + 1, nz - 1) + two() + two() + two() + two(2)
         + two(PARTS, nz) + two(PARTS, nz) + two(PARTS) + two(PARTS, 2) + two(PARTS, 4),
         compiler_params=params(cid),
         name="finish",
-    )(xs, qkv, mixed, lse, whole, segments, hidden, probs, places, inner, gin, res, cot, attended, dw_half)
+    )(xs, lse, whole, segments, hidden, probs, places, inner, qkv, mixed, gin, res, cot, attended, dw_half)
 
 
 def spread_kernel(in_ref, out_ref):
@@ -1216,7 +1232,7 @@
     hidden, probs, gin, res, inner, dw_half = experts(
         x, attended, whole, places_row, places_col, raw, near, capacity, nz, 1
     )
-    block_out, d_tokens, d_in, d_out, d_route, d_gains, _, _, dw_all = finish(
+    block_out, d_tokens, d_in, d_out, d_route, d_gains, dw_all = finish(
         xs, qkv, mixed, lse, whole, segments, hidden, probs, places_col, inner, gin, res, cot, attended, dw_half,
         prompt, nz, capacity, 2,
     )

time: 364 us -> 360 us (0.989)
  Pallas kernels: 341 us -> 337 us
    pallas_call x1, Pallas kernels: 152 us -> 148 us  [finish(): pl.pallas_call(functools.partial(finish_kernel, prompt, nz, capacity), ou...]
where the time goes in v3:
time: 360 us; the launch traced here: 356 us
  Pallas kernels  337 us (94%)
  local copies, waits for them, and re-layouts  17.8 us (5%)
    pallas_call x1, Pallas kernels, finish(): pl.pallas_call(functools.partial(finish_kernel, prompt, nz, capacity), ou...  148 us
    pallas_call x1, Pallas kernels, experts(): pl.pallas_call(functools.partial(experts_kernel, capacity, nz), out_shape...  101 us
    pallas_call x1, Pallas kernels, begin(): pl.pallas_call(functools.partial(begin_kernel, prompt, nz, capacity), out...  76.3 us
    unnamed x18, local copies, waits for them, and re-layouts  13.1 us
    pallas_call x1, Pallas kernels, spread_experts(): pl.pallas_call(spread_kernel, grid=(cores, r // block), out_shape=sds((co...  12 us

profile of v3, /device:TPU:9, one launch (start us, length us, event | category | flops | bytes accessed | tf_op | source)
XLA Modules:
  0.0 355.8 jit_solution(13689675989638953854)
XLA Ops:
  0.7 1.4 copy.23.router_ref
  2.1 1.4 copy.24.gains_ref
  3.5 1.6 copy.21
  5.1 4.8 %constant_dynamic-slice_fusion = bf16[384,1,1536]{2,1,0:T(2,128)(2,1)S(1)} fusion(bf16[768,4,1536]{2,1,0:T(4,128)(2,1)} %param.14, s32[]{:T(128)S(6)} %select_n.11, s32[]{:T(128)S(6)} %select_n.13), kind=kLoop, calls=%fused_computation.1 | loop fusion | bytes 2359304 | tf_op jit(solution)/shard_map/dynamic_slice | solution.py:1228
  9.9 1.2 copy.29
  11.1 76.3 %begin.1 = (bf16[1536,768]{1,0:T(8,128)(2,1)}, bf16[768,2048]{1,0:T(8,128)(2,1)}, bf16[3,3,1536,128]{3,2,1,0:T(8,128)(2,1)}, bf16[3,1536,128]{2,1,0:T(8,128)(2,1...) custom-call(bf16[768,768]{1,0:T(8,128)(2,1)} %bitcast.11, ...), custom_call_target="tpu_custom_call" | custom-call | tf_op jit(solution)/shard_map/begin/pallas_call | solution.py:351
  87.4 100.8 %experts.1 = (f32[768,768]{1,0:T(8,128)}, f32[768,128]{1,0:T(8,128)}, bf16[4,384,768]{2,1,0:T(8,128)(2,1)}, bf16[4,384,768]{2,1,0:T(8,128)(2,1)}, f32[4,8,384]{2,1,0:T(8,128)}, /*index=5*/bf16[4,384,1536]{2,1,0:T(8,128)(2,1)}) custom-call(bf16[768,768]{1,0:T(8,128)(2,1)} %bitcast.12, bf16[768,768]{1,0:T(8,128)(2,1)} %get-tuple-element.33.att_ref, ...), custom_call_target="tpu_custom_call" | custom-call | tf_op jit(solution)/shard_map/experts/pallas_call | solution.py:637
  188.1 148.0 %finish.1 = (bf16[768,768]{1,0:T(8,128)(2,1)}, bf16[768,768]{1,0:T(8,128)(2,1)}, f32[192,2304]{1,0:T(8,128)}, f32[192,768]{1,0:T(8,128)}, f32[192,4]{1,0:T(8,128...) custom-call(bf16[1536,768]{1,0:T(8,128)(2,1)} %get-tuple-element.30.xs_ref, ...), custom_call_target="tpu_custom_call" | custom-call | tf_op jit(solution)/shard_map/finish/pallas_call | solution.py:1145
  336.2 1.6 copy.26
  337.7 1.6 copy.25
  339.3 0.0 copy-start.2
  339.3 0.0 copy-start.1
  339.3 12.0 %spread.1 = f32[768,4,1536]{2,1,0:T(4,128)} custom-call(bf16[2,4,384,1536]{3,2,1,0:T(8,128)(2,1)} %get-tuple-element.52.in_ref), custom_call_target="tpu_custom_call" | custom-call | tf_op jit(solution)/shard_map/spread/pallas_call | solution.py:1204
  351.2 0.0 copy-done.2
  351.3 0.0 copy-start
  351.3 1.0 copy.34
  352.3 0.0 copy-done.1
  352.3 1.0 copy.35
  353.3 0.0 copy-done
  353.3 0.0 copy-start.3
  353.3 1.2 copy.36
  354.5 0.3 copy-done.3
  354.8 0.8 copy.37
Async XLA Ops:
  339.3 12.0 %copy-start.2 = (bf16[768,768]{1,0:T(8,128)(2,1)S(1)}, bf16[768,768]{1,0:T(8,128)(2,1)}, u32[]{:S(2)}) copy-start(bf16[768,768]{1,0:T(8,128)(2,1)} %get-tuple-element.46) | copy-start | bytes 3538948
  339.3 13.0 %copy-start.1 = (bf16[768,768]{1,0:T(8,128)(2,1)S(1)}, bf16[768,768]{1,0:T(8,128)(2,1)}, u32[]{:S(2)}) copy-start(bf16[768,768]{1,0:T(8,128)(2,1)} %get-tuple-element.47) | copy-start | bytes 3538948
  351.3 2.0 copy-start
  353.3 1.5 copy-start.3

commit v4 on v3

--- a/solution.py
+++ b/solution.py
@@ -155,6 +155,15 @@
     row = x.astype(F32)
     col = jnp.broadcast_to(row, (128, row.shape[1])).T[:, 0:1]
     return row, col
+
+
+def upright(rows, count):
+    wide = -(-count // 128) * 128
+    few = rows.astype(F32)
+    few = jnp.concatenate([few, jnp.zeros((8 - few.shape[0], count), F32)], axis=0)
+    if wide > count:
+        few = jnp.concatenate([few, jnp.zeros((8, wide - count), F32)], axis=1)
+    return few.T[0:count, :]
 
 
 def begin_kernel(
@@ -192,10 +201,11 @@
         c.start()
     lane = iota((1, 128), 1)
     small = jnp.zeros((shard, 128), F32)
+    router_cols, gain_cols = upright(router_ref[...], shard), upright(gains_ref[...], shard)
     for e in range(EXPERTS):
-        small = jnp.where(lane == e, router_ref[:, e : e + 1].astype(F32), small)
+        small = jnp.where(lane == e, router_cols[:, e : e + 1], small)
     for e in range(2):
-        small = jnp.where(lane == EXPERTS + e, gains_ref[:, e : e + 1].astype(F32), small)
+        small = jnp.where(lane == EXPERTS + e, gain_cols[:, e : e + 1], small)
     pack[:, own_cols:lead] = small.astype(BF)
     greet([sibling, partner, across] + others)
     tokens = remote(x_ref, xs_ref.at[pl.ds(base, rows)], send_t, recv_t, partner)
@@ -226,8 +236,9 @@
     own = pltpu.make_async_copy(pack, w_ref.at[pl.ds(pl.multiple_of(z * shard, shard), shard)], local.at[3 * pairs + 1])
     own.start()
     xs_ref[pl.ds(base, rows), :] = x_ref[...]
-    ids = ids_ref[...]
-    chosen = jnp.where((ids[:, 0:1] == lane) | (ids[:, 1:2] == lane), 1.0, 0.0)
+    ids = upright(ids_ref[...], rows)
+    lanes_f = lane.astype(F32)
+    chosen = jnp.where((ids[:, 0:1] == lanes_f) | (ids[:, 1:2] == lanes_f), 1.0, 0.0)
     earlier = (iota((rows, rows), 1) < iota((rows, rows), 0)).astype(F32).astype(BF)
     places = jnp.where(chosen > 0, nn(earlier, chosen.astype(BF)), -1.0)
     col_ref[...] = places
@@ -240,7 +251,6 @@
             over(d, g, x).start()
             beside(d, g, 0, core).start()
         if g == 0:
-            line.start(1)
             for d in range(1, nz):
                 along(d, 1).start()
         for d in range(1, nz):
@@ -257,6 +267,7 @@
     line = Line(
         nz, dp, sq, z, lambda stage, zone: piece_ref if stage == 1 else near_ref.at[zone], near_ref, line_sems
     )
+    line.start(1)
     gather(0)
     gathered(0)
     own.wait()
@@ -280,6 +291,9 @@
         return remote(
             src, att_ref.at[:, pl.ds(al(side * half + p * 128), 128)], send_o.at[p], recv_o.at[p], partner
         )
+
+    line.wait_recv(1)
+    line.start(2)
 
     @pl.loop(0, pairs)
     def _(p):
@@ -317,8 +331,6 @@
 
         @pl.when(p == 0)
         def _():
-            line.wait_recv(1)
-            line.start(2)
             gather(1)
 
     for j, (px, py) in enumerate([flip_chip(x, sq, *f) for f in SOURCES]):
@@ -1104,8 +1116,10 @@
     pass_on(1 - x, 1 - core, send_b.at[1], recv_b.at[1], sibling).wait_recv()
     din_out[...] = total[:, 0 : 3 * width].astype(F32)
     small = total[:, 3 * width : 3 * width + 128].astype(F32)
-    droute_out[...] = small[:, 0:EXPERTS]
-    dgains_out[...] = small[:, EXPERTS : EXPERTS + 2]
+    wide = -(-shard // 128) * 128
+    turned = jnp.concatenate([small, jnp.zeros((wide - shard, 128), F32)], axis=0).T
+    droute_out[...] = turned[0:EXPERTS, 0:shard]
+    dgains_out[...] = turned[EXPERTS : EXPERTS + 2, 0:shard]
     dout_out[...] = total[:, 3 * width + 128 :].astype(F32)
     last_part(3)
     end_parts()
@@ -1149,8 +1163,8 @@
             sds((rows, width), BF),
             sds((shard, 3 * width), F32),
             sds((shard, width), F32),
-            sds((shard, EXPERTS), F32),
-            sds((shard, 2), F32),
+            sds((EXPERTS, shard), F32),
+            sds((2, shard), F32),
             sds((2, 4) + dw_half.shape[1:], BF),
         ),
         in_specs=[VM] * 8 + [ANY] * 7,
@@ -1227,7 +1241,7 @@
     part = expert_w.shape[0] // 2
     piece = lax.dynamic_slice(expert_w, (core * part, mine, 0), (part, 1, 2 * width))[:, 0]
     xs, whole, qkv, mixed, lse, attended, raw, places_row, places_col, near = begin(
-        x, attn_in, attn_out, router, gains, segments, expert_ids[0], cot, piece, prompt, nz, capacity, 0
+        x, attn_in, attn_out, router.T, gains.T, segments, expert_ids[0].T, cot, piece, prompt, nz, capacity, 0
     )
     hidden, probs, gin, res, inner, dw_half = experts(
         x, attended, whole, places_row, places_col, raw, near, capacity, nz, 1
@@ -1242,8 +1256,8 @@
         d_tokens[None],
         d_in,
         d_out,
-        d_route,
-        d_gains,
+        d_route.T,
+        d_gains.T,
         d_expert,
     )
 

time: 360 us -> 353 us (0.981)
  local copies, waits for them, and re-layouts: 17.8 us -> 11.4 us
    unnamed x18 -> x19, local copies, waits for them, and re-layouts: 13.1 us -> 6.63 us
where the time goes in v4:
time: 353 us; the launch traced here: 349 us
  Pallas kernels  337 us (95%)
  local copies, waits for them, and re-layouts  11.4 us (3%)
    pallas_call x1, Pallas kernels, finish(): pl.pallas_call(functools.partial(finish_kernel, prompt, nz, capacity), ou...  148 us
    pallas_call x1, Pallas kernels, experts(): pl.pallas_call(functools.partial(experts_kernel, capacity, nz), out_shape...  99.1 us
    pallas_call x1, Pallas kernels, begin(): pl.pallas_call(functools.partial(begin_kernel, prompt, nz, capacity), out...  77.9 us
    pallas_call x1, Pallas kernels, spread_experts(): pl.pallas_call(spread_kernel, grid=(cores, r // block), out_shape=sds((co...  12 us

profile of v4, /device:TPU:9, one launch (start us, length us, event | category | flops | bytes accessed | tf_op | source)
XLA Modules:
  0.0 349.1 jit_solution(9247612982602835263)
XLA Ops:
  0.7 4.8 %constant_dynamic-slice_fusion = bf16[384,1,1536]{2,1,0:T(2,128)(2,1)S(1)} fusion(bf16[768,4,1536]{2,1,0:T(4,128)(2,1)} %param.14, s32[]{:T(128)S(6)} %select_n.11, s32[]{:T(128)S(6)} %select_n.13), kind=kLoop, calls=%fused_computation.1 | loop fusion | bytes 2359304 | tf_op jit(solution)/shard_map/dynamic_slice | solution.py:1242
  5.4 1.2 copy.19
  6.6 77.9 %begin.1 = (bf16[1536,768]{1,0:T(8,128)(2,1)}, bf16[768,2048]{1,0:T(8,128)(2,1)}, bf16[3,3,1536,128]{3,2,1,0:T(8,128)(2,1)}, bf16[3,1536,128]{2,1,0:T(8,128)(2,1...) custom-call(bf16[768,768]{1,0:T(8,128)(2,1)} %bitcast.17, ...), custom_call_target="tpu_custom_call" | custom-call | tf_op jit(solution)/shard_map/begin/pallas_call | solution.py:363
  84.5 99.1 %experts.1 = (f32[768,768]{1,0:T(8,128)}, f32[768,128]{1,0:T(8,128)}, bf16[4,384,768]{2,1,0:T(8,128)(2,1)}, bf16[4,384,768]{2,1,0:T(8,128)(2,1)}, f32[4,8,384]{2,1,0:T(8,128)}, /*index=5*/bf16[4,384,1536]{2,1,0:T(8,128)(2,1)}) custom-call(bf16[768,768]{1,0:T(8,128)(2,1)} %bitcast.18, bf16[768,768]{1,0:T(8,128)(2,1)} %get-tuple-element.33.att_ref, ...), custom_call_target="tpu_custom_call" | custom-call | tf_op jit(solution)/shard_map/experts/pallas_call | solution.py:649
  183.7 147.8 %finish.1 = (bf16[768,768]{1,0:T(8,128)(2,1)}, bf16[768,768]{1,0:T(8,128)(2,1)}, f32[192,2304]{1,0:T(8,128)}, f32[192,768]{1,0:T(8,128)}, f32[4,192]{1,0:T(4,128...) custom-call(bf16[1536,768]{1,0:T(8,128)(2,1)} %get-tuple-element.30.xs_ref, ...), custom_call_target="tpu_custom_call" | custom-call | tf_op jit(solution)/shard_map/finish/pallas_call | solution.py:1159
  331.4 0.0 copy-start.2
  331.4 0.0 copy-start.1
  331.5 12.0 %spread.1 = f32[768,4,1536]{2,1,0:T(4,128)} custom-call(bf16[2,4,384,1536]{3,2,1,0:T(8,128)(2,1)} %get-tuple-element.52.in_ref), custom_call_target="tpu_custom_call" | custom-call | tf_op jit(solution)/shard_map/spread/pallas_call | solution.py:1218
  343.4 0.0 copy-done.2
  343.5 0.0 copy-start
  343.5 1.0 copy.26
  344.5 0.0 copy-done.1
  344.5 1.0 copy.27
  345.5 0.0 copy-done
  345.5 0.0 copy-start.3
  345.5 0.0 copy-start.4
  345.5 0.0 copy-start.5
  345.5 1.2 copy.28
  346.7 0.2 copy-done.3
  346.9 0.8 copy.29
  347.7 0.0 copy-done.4
  347.7 0.6 copy.30
  348.3 0.0 copy-done.5
  348.3 0.6 copy.31
Async XLA Ops:
  331.4 12.0 %copy-start.2 = (bf16[768,768]{1,0:T(8,128)(2,1)S(1)}, bf16[768,768]{1,0:T(8,128)(2,1)}, u32[]{:S(2)}) copy-start(bf16[768,768]{1,0:T(8,128)(2,1)} %get-tuple-element.46) | copy-start | bytes 3538948
  331.4 13.0 %copy-start.1 = (bf16[768,768]{1,0:T(8,128)(2,1)S(1)}, bf16[768,768]{1,0:T(8,128)(2,1)}, u32[]{:S(2)}) copy-start(bf16[768,768]{1,0:T(8,128)(2,1)} %get-tuple-element.47) | copy-start | bytes 3538948
  343.5 2.0 copy-start
  345.5 1.4 copy-start.3
  345.5 2.3 copy-start.4
  345.5 2.9 copy-start.5
